TPU v7x, 32 devices: a whole 2x2x4 slice. The times are simulated.
32 devices in a mesh: freq: 8 (over y, x, core), rcv: 4 (over z).
Axes of the slice: x: 2, y: 2, z: 4, core: 2. Of those that a mesh axis runs over, the one named last changes fastest.
Arguments:
- kernel: float32 [2, 128, 1024, 1024], P(None, 'freq', 'rcv'), may hold values from -2 to 2, as said below
- focus_start: float32 [8, 1024, 512], P('freq', 'rcv'), may hold values from -6 to 6
- onset: int32 [8, 1024], P('freq', 'rcv'), may hold values from 64 to 447
- freq_order: int32 [128], replicated, may hold values from 0 to 127, each once
Outputs:
- focusing: float32 [8, 1024, 512], P('freq', 'rcv')
- downgoing: float32 [8, 1024, 512], P('freq', 'rcv')
Inputs may be any that keep to these rules, and one draw needn't show every extreme that they name: kernel[c,k,s,r] equals kernel[c,k,r,s] exactly (reciprocity).
All inputs are finite; a program needn't handle non-finite values.
Results may differ from a plain program's by a relative error of at most 0.0001.
Values sent between devices are 32-bit elements; how exact they have to be, the bound alone decides.
No kernel may reach another device: no remote copies, remote signals or barrier semaphores. Data moves between devices by JAX's collectives and lax.ppermute only.
A program may use at most 128 MiB of HBM per device.

v0:
```python
import functools
import math

import jax
import jax.numpy as jnp
from jax import lax
from jax.experimental import pallas as pl
from jax.experimental.pallas import tpu as pltpu
from jax.sharding import PartitionSpec as P


ITERS = 2
F32, BF16 = jnp.float32, jnp.bfloat16
VMEM = pl.BlockSpec(memory_space=pltpu.VMEM)
HBM = pl.BlockSpec(memory_space=pltpu.HBM)


def call(body, ins, outs, args, mib=8, alias=None, scratch=()):
    return pl.pallas_call(
        body,
        in_specs=ins,
        out_specs=tuple(VMEM for _ in outs),
        out_shape=tuple(outs),
        scratch_shapes=scratch,
        input_output_aliases=alias or {},
        compiler_params=pltpu.CompilerParams(vmem_limit_bytes=mib << 20),
    )(*args)


def halves(x):
    high = x.astype(BF16)
    return high, (x - high.astype(F32)).astype(BF16)


def dot(a, b, left, right):
    return lax.dot_general(a, b, (((left,), (right,)), ((), ())), preferred_element_type=F32)


def dot3(a, b, left, right):
    return (
        dot(a[0], b[0], left, right) + dot(a[0], b[1], left, right) + dot(a[1], b[0], left, right)
    )


def column(row, length, place):
    shape = (length, row.shape[1])
    hit = place(lax.broadcasted_iota(jnp.int32, shape, 0))
    hit = hit == lax.broadcasted_iota(jnp.int32, shape, 1)
    return jnp.sum(jnp.where(hit, row.astype(F32), 0.0), axis=1, keepdims=True)


def cosine(turn):
    x = (2.0 * math.pi) * (0.25 - jnp.minimum(turn, 1.0 - turn))
    square = x * x
    series = 0.0
    for power in range(13, 0, -2):
        series = series * square + (-1.0) ** (power // 2) / math.factorial(power)
    return series * x


def make_table(order, me, n, th, tl, scale):
    rows, samples = th.shape
    shape = (rows, samples)
    time = lax.broadcasted_iota(jnp.int32, shape, 1).astype(F32) / samples
    part = (lax.broadcasted_iota(jnp.int32, shape, 0) & 1).astype(F32) * 0.25

    def slot(r):
        return jnp.bitwise_xor(lax.div(r, 2 * n), me) * n + lax.rem(lax.div(r, 2), n)

    q = column(order, rows, slot)
    scale[...] = jnp.where(q == 0.0, 1.0, 2.0) / samples
    turn = q * time + part
    table = halves(cosine(turn - jnp.floor(turn)))
    th[...] = table[0]
    tl[...] = table[1]
    return table


def spectrum_body(n, order_in, onset_in, x_in, me, th, tl, scale, limit, *rest):
    *outs, order, onset, x, sems = rest
    pairs = ((order_in, order), (onset_in, onset), (x_in, x))
    copies = [pltpu.make_async_copy(a, b, sems.at[i]) for i, (a, b) in enumerate(pairs)]
    for copy in copies:
        copy.start()
    copies[0].wait()
    table = make_table(order[...], me[0], n, th, tl, scale)
    copies[1].wait()
    limit[...] = column(onset[...], limit.shape[0], lambda r: r).astype(jnp.int32)
    copies[2].wait()
    y = dot3(table, halves(x[...]), 1, 1)
    if len(outs) == 1:
        outs[0][...] = y
        return
    step = 2 * n
    for j in range(y.shape[0] // step):
        outs[j % 2][j // 2] = y[j * step : (j + 1) * step]


def pair_body(keep, given, limit, onset, both, *outs):
    both[0] = limit[...]
    both[1] = column(onset[...], limit.shape[0], lambda r: r).astype(jnp.int32)
    for q, out in enumerate(outs):
        out[0] = keep[q]
        out[1] = given[q]


def pair_mute_body(chips, last, base, scale, onset, th, tl, *rest):
    own, other, rest = rest[:chips], rest[chips : 2 * chips], list(rest[2 * chips :])
    base = [rest.pop(0) for _ in range(base)]
    points = 1 if last else 2
    step = own[0].shape[1]
    fields = []
    for j in range(points):
        parts = [x[i] for q in range(chips) for x, i in ((own[q], j), (other[q], 1 - j))]
        fields.append((jnp.concatenate(parts, axis=0) * scale[...]).T)
    y = dot3(halves(jnp.concatenate(fields, axis=0)), (th[...], tl[...]), 1, 0)
    t = lax.broadcasted_iota(jnp.int32, y.shape, 1)
    limit = jnp.concatenate([onset[j] for j in range(points)], axis=0)
    y = jnp.where(t < limit, y, 0.0)
    if last:
        rest[0][...] = base[0][...] + y if base else y
        return
    mine = [
        jnp.concatenate([x[2 * q * step : (2 * q + 1) * step, :] for q in range(chips)], axis=0)
        for x in (th, tl)
    ]
    z = dot3(mine, halves(y), 1, 1)
    width = z.shape[1] // 2
    for q, out in enumerate(rest):
        for j in range(2):
            piece = z[q * step : (q + 1) * step, j * width : (j + 1) * width]
            out[j] = base[q][j] + piece if base else piece


def pack_body(chips, *rest):
    pieces, outs = rest[:chips], rest[chips:]
    for q, piece in enumerate(pieces):
        outs[0][pl.ds(2 * q, 2)] = piece[...]
        for i, out in enumerate(outs[1:]):
            half = out.shape[1]
            out[pl.ds(2 * q, 2)] = piece[:, i * half : (i + 1) * half, :]


def mute_body(last, add, scale, onset, product, th, tl, *rest):
    table = (th[...], tl[...])
    y = dot3(halves((product[...] * scale[...]).T), table, 1, 0)
    t = lax.broadcasted_iota(jnp.int32, y.shape, 1)
    y = jnp.where(t < onset[...], y, 0.0)
    if not last:
        y = dot3(table, halves(y), 1, 1)
    rest[-1][...] = rest[0][...] + y if add else y


def fill(field, arrays, at):
    span, rows = field.shape[0] * 2, field.shape[3]
    for i in range(arrays[0].shape[0]):
        field[:, :, i, :] = arrays[0][i, 2 * at : 2 * at + span, :].reshape(-1, 2, rows)
    for i in range(arrays[1].shape[0]):
        field[:, :, 2 + i, :] = arrays[1][i].reshape(-1, 2, rows)


def share(x, weights):
    h, l = halves(x)
    both = jnp.concatenate([h, l], axis=0)
    rows = x.shape[0]
    out = []
    for high, low in weights:
        p = dot(both, high, 1, 0)
        out.append(p[:rows] + p[rows:] + dot(h, low, 1, 0))
    return out


def combine(parts, parity, v):
    return (
        parts[0][:v] - parity * parts[1][v:],
        parity * parts[1][:v] + parts[0][v:],
    )


def hold_body(blocks, parity, width, kernel, place, *rest):
    arrays, rest = rest[:width], rest[width:]
    outs, (total, buf, sem), scratch = rest[: 2 * blocks], rest[2 * blocks :][:3], rest[2 * blocks + 3 :]
    n, rows = kernel.shape[1:3]
    slots = buf.shape[0]

    def copy(k):
        slot = lax.rem(k, slots)
        return pltpu.make_async_copy(kernel.at[:, k], buf.at[slot], sem.at[slot])

    for k in range(min(slots - 1, n)):
        copy(k).start()
    field = arrays[0]
    if width > 1:
        field = scratch[0]
        fill(field, arrays, 0)
    v = field.shape[2]

    @pl.loop(0, n)
    def _(k):
        @pl.when(k + slots - 1 < n)
        def _():
            copy(k + slots - 1).start()

        copy(k).wait()
        slot = lax.rem(k, slots)
        weights = []
        for b in range(blocks):
            col = pl.multiple_of(jnp.bitwise_xor(place[0], b) * rows, rows)
            for c in range(2):
                x = buf[slot, c, :, pl.ds(col, rows)]
                h, l = halves(x if b == 0 else x.T)
                outs[2 * b][c, k] = h
                outs[2 * b + 1][c, k] = l
                if b == 0:
                    weights.append((h, l))
        sums = combine(share(field[k].reshape(2 * v, rows), weights), parity, v)
        for c in range(2):
            total[k, c] = sums[c]


def product_body(parity, pieces, first, chips, widths, *rest):
    count = len(pieces)
    highs, lows, rest = rest[:count], rest[count : 2 * count], list(rest[2 * count :])
    given = [[rest.pop(0) for _ in range(width)] for width in widths]
    total = None if first else rest.pop(0)
    outs = [rest.pop(0) for _ in range(max(1, chips))]
    n = (outs[0] if first else total).shape[0]
    fields = []
    for (_, at), arrays in zip(pieces, given):
        if len(arrays) == 1:
            fields.append(arrays[0])
            continue
        fields.append(rest.pop(0))
        fill(fields[-1], arrays, at)
    v, rows = fields[0].shape[2:]
    cuts = {0, n} | {at for _, at in pieces}
    cuts = sorted(cuts | {at + x.shape[0] for (_, at), x in zip(pieces, fields)})

    def one(k, here):
        parts = None
        for high, low, at, x in here:
            weights = [(high[c, k], low[c, k]) for c in range(2)]
            p = share(x[k - at].reshape(2 * v, rows), weights)
            parts = p if parts is None else [i + j for i, j in zip(parts, p)]
        sums = [None, None] if parts is None else list(combine(parts, parity, v))
        for c in range(2):
            if not first:
                sums[c] = total[k, c] if sums[c] is None else total[k, c] + sums[c]
            if not chips:
                outs[0][k, c] = sums[c]
                continue
            for i in range(v):
                outs[i // 2][i % 2, pl.ds(2 * k + c, 1), :] = sums[c][i : i + 1]

    for begin, end in zip(cuts[:-1], cuts[1:]):
        here = [
            (high, low, at, x)
            for (_, at), high, low, x in zip(pieces, highs, lows, fields)
            if at <= begin and end <= at + x.shape[0]
        ]
        if not here and not chips:
            continue
        step = math.gcd(end - begin, max(1, 8 // max(1, len(here))))

        @pl.loop(begin // step, end // step)
        def _(i):
            for j in range(step):
                one(i * step + j, here)


def body(z_size, kernel, focus_start, onset, freq_order):
    sds = jax.ShapeDtypeStruct
    _, n, rows, receivers = kernel.shape
    own, samples = focus_start.shape[0], focus_start.shape[2]
    n_f = freq_order.shape[0] // n
    points = n_f * own
    chips = 4 if n_f == 8 and own == 1 and n % 2 == 0 and z_size == 4 else 0
    place = lax.axis_index("rcv")[None].astype(jnp.int32)
    me = lax.axis_index("freq")[None].astype(jnp.int32) * (1 if chips else 0)
    smem = pl.BlockSpec(memory_space=pltpu.SMEM)

    n_rows = 2 * freq_order.shape[0]
    traces = focus_start.reshape(own * rows, samples)
    if chips:
        spectra = [sds((chips, 2 * n, rows), F32)] * 2
    else:
        spectra = [sds((n_rows, own * rows), F32)]
    th, tl, scale, limit, *start = call(
        functools.partial(spectrum_body, n),
        [HBM] * 3 + [smem],
        [sds((n_rows, samples), BF16)] * 2
        + [sds((n_rows, 1), F32), sds((own * rows, 1), jnp.int32)]
        + spectra,
        [
            pltpu.with_memory_space_constraint(x, pltpu.HBM)
            for x in (freq_order.reshape(1, -1), onset.reshape(1, -1), traces)
        ]
        + [me],
        scratch=[
            pltpu.VMEM((1, n_rows // 2), jnp.int32),
            pltpu.VMEM((1, own * rows), jnp.int32),
            pltpu.VMEM((own * rows, samples), F32),
            pltpu.SemaphoreType.DMA((3,)),
        ],
    )

    def trade(x, d):
        return lax.ppermute(x, "freq", [(i, i ^ d) for i in range(n_f)])

    def across(pieces):
        moved = {q: trade(pieces[q], 2 * q) for q in (3, 1, 2)}
        return [pieces[0]] + [moved[q] for q in (1, 2, 3)]

    if chips:
        given = trade(start[1], 1)
        limit, *start = call(
            pair_body,
            [VMEM] * 4,
            [sds((2, rows, 1), jnp.int32)] + [sds((2, 2 * n, rows), F32)] * chips,
            (start[0], given, limit, trade(onset, 1)),
        )
    else:
        start = start[0]

    held = None

    def shift(x, d):
        return lax.ppermute(x, "rcv", [(i, i ^ d) for i in range(z_size)])

    def gather(near, x, low=None, high=None):
        if z_size != 4 or n % 2 or held is None:
            far = {d: shift(x, d) for d in range(1, z_size)}
            pieces = [(0, 0, x)] + [(d, 0, far[d]) for d in far]
        else:
            half = n // 2
            b0 = shift(low, 2)
            a = shift(x, 1)
            c1 = shift(high, 3)
            b1 = shift(high, 2)
            c0 = shift(b0, 1)
            pieces = [(0, 0, x), (2, 0, b0), (1, 0, a), (3, half, c1), (3, 0, c0), (2, half, b1)]
        return [
            [(b, at, [near[b], array] if near else [array])] for b, at, array in pieces
        ]

    def field_scratch(arrays):
        if len(arrays) == 1:
            return []
        return [pltpu.VMEM((arrays[1].shape[1] // 2, 2, points, rows), F32)]

    def hold(arrays, parity):
        shape = (2, n, rows, rows)
        *outs, total = pl.pallas_call(
            functools.partial(hold_body, z_size, parity, len(arrays)),
            in_specs=[HBM, smem] + [VMEM] * len(arrays),
            out_specs=(VMEM,) * (2 * z_size + 1),
            out_shape=(pltpu.VMEM(shape, BF16),) * (2 * z_size)
            + (sds((n, 2, points, rows), F32),),
            scratch_shapes=[pltpu.VMEM((4, 2, rows, receivers), F32), pltpu.SemaphoreType.DMA((4,))]
            + field_scratch(arrays),
            compiler_params=pltpu.CompilerParams(vmem_limit_bytes=12 << 20),
        )(kernel, place, *arrays)
        return outs, [total]

    def product(spectrum, parity):
        nonlocal held
        if chips:
            pieces = across(spectrum)
            near = [pieces[0]] + [shift(pieces[0], d) for d in range(1, z_size)]
            far = points - 2
            shapes = [(far, 2 * n, rows)] + ([(far, n, rows)] * 2 if held else [])
            packed = call(
                functools.partial(pack_body, chips - 1),
                [VMEM] * (chips - 1),
                [sds(shape, F32) for shape in shapes],
                pieces[1:],
            )
            groups = gather(near, *packed)
        else:
            s = spectrum.reshape(n_f, 2 * n, own, rows)
            x = lax.all_to_all(s, "freq", split_axis=0, concat_axis=0, tiled=True)
            x = x.reshape(n_f, n, 2, own, rows).transpose(1, 2, 0, 3, 4)
            x = x.reshape(n, 2, points, rows)
            groups = gather(None, x, x[: n // 2], x[n // 2 :])
        total = None
        if held is None:
            held, total = hold(groups.pop(0)[0][2], parity)
        for step, group in enumerate(groups):
            args = [held[2 * b + h] for h in (0, 1) for b, _, _ in group]
            widths = [len(arrays) for _, _, arrays in group]
            args += [x for _, _, arrays in group for x in arrays]
            scratch = [x for _, _, arrays in group for x in field_scratch(arrays)]
            first, end = total is None, chips if step == len(groups) - 1 else 0
            outs = [sds((2, 2 * n, rows), F32)] * end or [sds((n, 2, points, rows), F32)]
            if not first:
                args += total
            pieces = [piece[:2] for piece in group]
            total = call(
                functools.partial(product_body, parity, pieces, first, end, widths),
                [VMEM] * len(args),
                outs,
                args,
                scratch=scratch,
                alias=None if first or end else {len(args) - 1: 0},
            )
        if chips:
            back = across(total)
            return back + [trade(x, 1) for x in back]
        back = total[0].reshape(2 * n, n_f, own, rows).transpose(1, 0, 2, 3)
        back = lax.all_to_all(back, "freq", split_axis=0, concat_axis=0, tiled=True)
        return back.reshape(n_rows, own * rows)

    def mute(back, last, base):
        if chips:
            base = [] if base is None else [base] if last else base
            outs = [sds((rows, samples), F32)] if last else [sds((2, 2 * n, rows), F32)] * chips
            args = (scale, limit, th, tl, *back, *base)
            body = functools.partial(pair_mute_body, chips, last, len(base))
            got = call(body, [VMEM] * len(args), outs, args)
            return got[0] if last else got
        outs = [sds((own * rows, samples) if last else (n_rows, own * rows), F32)]
        args = (scale, limit, back, th, tl) + (() if base is None else (base,))
        body = functools.partial(mute_body, last, base is not None)
        return call(body, [VMEM] * len(args), outs, args)[0]

    field = start
    for iteration in range(ITERS):
        final = iteration == ITERS - 1
        back = product(field, 1.0)
        field = mute(back, False, None)
        if final:
            downgoing = mute(back, True, None)
        back = product(field, -1.0)
        field = mute(back, final, traces if final else start)
    return field.reshape(focus_start.shape), downgoing.reshape(focus_start.shape)


def solution(mesh):
    in_specs = (P(None, "freq", "rcv", None), P("freq", "rcv", None), P("freq", "rcv"), P())
    out_specs = (P("freq", "rcv", None), P("freq", "rcv", None))
    return jax.shard_map(
        functools.partial(body, mesh.shape["rcv"]),
        mesh=mesh,
        in_specs=in_specs,
        out_specs=out_specs,
        check_vma=False,
    )
```

profile of v0, /device:TPU:0, one launch (start us, length us, event | category | flops | bytes accessed | tf_op | source)
XLA Modules:
  0.0 177.2 jit_solution(16645551662504544002)
XLA Ops:
  0.6 2.1 %shard_map.59 = (bf16[256,512]{1,0:T(8,128)(2,1)S(1)}, bf16[256,512]{1,0:T(8,128)(2,1)S(1)}, f32[256,1]{1,0:T(8,128)S(1)}, s32[256,1]{1,0:T(8,128)S(1)}, f32[4,3...) custom-call(s32[1,128]{1,0:T(1,128)} %bitcast.10, s32[1,256]{1,0:T(1,128)} %onset_in.1, f32[256,512]{1,0:T(8,128)} %bitcast.6, ...), custom_call_target="tpu_custom_call" | custom-call | tf_op jit(solution)/shard_map/pallas_call | solution.py:19
  4.8 2.7 %collective-permute-start.2 = (f32[2,32,256]{2,1,0:T(8,128)S(1)}, f32[2,32,256]{2,1,0:T(8,128)S(1)}, u32[]{:S(2)}, u32[]{:S(2)}) collective-permute-start(f32[2,32,256]{2,1,0:T(8,128)S(1)} %get-tuple-element.67.rest_9_), channel_id=1, source_target_pairs={{0,8},{4,12},{8,0},{12,4},{16,24},{20,28},{24,16},{28,20},{1,9},{5... | collective-permute-start | bytes 196616 | tf_op jit(solution)/shard_map/ppermute | solution.py:308
  11.8 2.4 %collective-permute-done.4.rest_2_ = f32[2,32,256]{2,1,0:T(8,128)S(1)} collective-permute-done((f32[2,32,256]{2,1,0:T(8,128)S(1)}, f32[2,32,256]{2,1,0:T(8,128)S(1)}, u32[]{:S(2)}, u32[]{:S(2)}) %collective-permute-start.4) | collective-permute-done | bytes 65568 | tf_op jit(solution)/shard_map/ppermute | solution.py:308
  15.9 2.6 %collective-permute-start.8 = (f32[6,32,256]{2,1,0:T(8,128)S(1)}, f32[6,32,256]{2,1,0:T(8,128)S(1)}, u32[]{:S(2)}, u32[]{:S(2)}) collective-permute-start(f32[6,32,256]{2,1,0:T(8,128)S(1)} %shard_map.61.rest_1_), channel_id=1, source_target_pairs={{0,2},{1,3},{2,0},{3,1},{4,6},{5,7},{6,4},{7,5},{8,10},{9,11},{10,... | collective-permute-start | bytes 589832 | tf_op jit(solution)/shard_map/ppermute | solution.py:328
  19.3 3.5 %collective-permute-start.7 = (f32[2,32,256]{2,1,0:T(8,128)S(1)}, f32[2,32,256]{2,1,0:T(8,128)S(1)}, u32[]{:S(2)}, u32[]{:S(2)}) collective-permute-start(f32[2,32,256]{2,1,0:T(8,128)S(1)} %get-tuple-element.66.rest_0_.rest_8_), channel_id=1, source_target_pairs={{0,2},{1,3},{2,0},{3,1},{4,6},{5,7},{6,4},{7,5},{8,10},{9,11},{10,... | collective-permute-start | bytes 196616 | tf_op jit(solution)/shard_map/ppermute | solution.py:328
  22.8 7.3 %collective-permute-done.9.rest_2_ = f32[2,32,256]{2,1,0:T(8,128)S(1)} collective-permute-done((f32[2,32,256]{2,1,0:T(8,128)S(1)}, f32[2,32,256]{2,1,0:T(8,128)S(1)}, u32[]{:S(2)}, u32[]{:S(2)}) %collective-permute-start.9) | collective-permute-done | bytes 65568 | tf_op jit(solution)/shard_map/ppermute | solution.py:328
  30.1 2.4 %collective-permute-start.5 = (f32[2,32,256]{2,1,0:T(8,128)S(1)}, f32[2,32,256]{2,1,0:T(8,128)S(1)}, u32[]{:S(2)}, u32[]{:S(2)}) collective-permute-start(f32[2,32,256]{2,1,0:T(8,128)S(1)} %get-tuple-element.66.rest_0_.rest_8_), channel_id=1, source_target_pairs={{0,3},{1,2},{2,1},{3,0},{4,7},{5,6},{6,5},{7,4},{8,11},{9,10},{10,... | collective-permute-start | bytes 196616 | tf_op jit(solution)/shard_map/ppermute | solution.py:328
  32.5 11.4 %shard_map.62 = (bf16[2,16,256,256]{3,2,1,0:T(8,128)(2,1)S(1)}, bf16[2,16,256,256]{3,2,1,0:T(8,128)(2,1)S(1)}, bf16[2,16,256,256]{3,2,1,0:T(8,128)(2,1)S(1)}, bf...) custom-call(f32[2,16,256,1024]{3,2,1,0:T(8,128)} %kernel.1, ...), custom_call_target="tpu_custom_call" | custom-call | tf_op jit(solution)/shard_map/pallas_call | solution.py:353
  49.8 2.3 %collective-permute-start.13 = (f32[2,32,256]{2,1,0:T(8,128)S(1)}, f32[2,32,256]{2,1,0:T(8,128)S(1)}, u32[]{:S(2)}, u32[]{:S(2)}) collective-permute-start(f32[2,32,256]{2,1,0:T(8,128)S(1)} %get-tuple-element.80), channel_id=1, source_target_pairs={{0,24},{4,28},{8,16},{12,20},{16,8},{20,12},{24,0},{28,4},{1,25},{... | collective-permute-start | bytes 196616 | tf_op jit(solution)/shard_map/ppermute | solution.py:308
  63.5 2.3 %collective-permute-done.21.rest_2_ = f32[2,32,256]{2,1,0:T(8,128)S(1)} collective-permute-done((f32[2,32,256]{2,1,0:T(8,128)S(1)}, f32[2,32,256]{2,1,0:T(8,128)S(1)}, u32[]{:S(2)}, u32[]{:S(2)}) %collective-permute-start.21) | collective-permute-done | bytes 65568 | tf_op jit(solution)/shard_map/ppermute | solution.py:308
  67.8 2.6 %collective-permute-start.18 = (f32[2,32,256]{2,1,0:T(8,128)S(1)}, f32[2,32,256]{2,1,0:T(8,128)S(1)}, u32[]{:S(2)}, u32[]{:S(2)}) collective-permute-start(f32[2,32,256]{2,1,0:T(8,128)S(1)} %get-tuple-element.81.rest_2_), channel_id=1, source_target_pairs={{0,2},{1,3},{2,0},{3,1},{4,6},{5,7},{6,4},{7,5},{8,10},{9,11},{10,... | collective-permute-start | bytes 196616 | tf_op jit(solution)/shard_map/ppermute | solution.py:328
  72.2 2.7 %collective-permute-done.24.rest_3_ = f32[6,16,256]{2,1,0:T(8,128)S(1)} collective-permute-done((f32[6,16,256]{2,1,0:T(8,128)S(1)}, f32[6,16,256]{2,1,0:T(8,128)S(1)}, u32[]{:S(2)}, u32[]{:S(2)}) %collective-permute-start.24) | collective-permute-done | bytes 98336 | tf_op jit(solution)/shard_map/ppermute | solution.py:328
  74.9 2.4 %collective-permute-start.25 = (f32[6,16,256]{2,1,0:T(8,128)S(1)}, f32[6,16,256]{2,1,0:T(8,128)S(1)}, u32[]{:S(2)}, u32[]{:S(2)}) collective-permute-start(f32[6,16,256]{2,1,0:T(8,128)S(1)} %collective-permute-done.24.rest_3_), channel_id=1, source_target_pairs={{0,1},{1,0},{2,3},{3,2},{4,5},{5,4},{6,7},{7,6},{8,9},{9,8},{10,11... | collective-permute-start | bytes 294920 | tf_op jit(solution)/shard_map/ppermute | solution.py:328
  89.3 2.3 %collective-permute-start.31 = (f32[2,32,256]{2,1,0:T(8,128)S(1)}, f32[2,32,256]{2,1,0:T(8,128)S(1)}, u32[]{:S(2)}, u32[]{:S(2)}) collective-permute-start(f32[2,32,256]{2,1,0:T(8,128)S(1)} %get-tuple-element.93), channel_id=1, source_target_pairs={{0,24},{4,28},{8,16},{12,20},{16,8},{20,12},{24,0},{28,4},{1,25},{... | collective-permute-start | bytes 196616 | tf_op jit(solution)/shard_map/ppermute | solution.py:308
  102.9 2.3 %collective-permute-done.39.rest_2_ = f32[2,32,256]{2,1,0:T(8,128)S(1)} collective-permute-done((f32[2,32,256]{2,1,0:T(8,128)S(1)}, f32[2,32,256]{2,1,0:T(8,128)S(1)}, u32[]{:S(2)}, u32[]{:S(2)}) %collective-permute-start.39) | collective-permute-done | bytes 65568 | tf_op jit(solution)/shard_map/ppermute | solution.py:308
  105.3 2.1 %collective-permute-start.46 = (f32[6,32,256]{2,1,0:T(8,128)S(1)}, f32[6,32,256]{2,1,0:T(8,128)S(1)}, u32[]{:S(2)}, u32[]{:S(2)}) collective-permute-start(f32[6,32,256]{2,1,0:T(8,128)S(1)} %get-tuple-element.100.rest_3_), channel_id=1, source_target_pairs={{0,1},{1,0},{2,3},{3,2},{4,5},{5,4},{6,7},{7,6},{8,9},{9,8},{10,11... | collective-permute-start | bytes 589832 | tf_op jit(solution)/shard_map/ppermute | solution.py:328
  107.7 2.6 %collective-permute-start.36 = (f32[2,32,256]{2,1,0:T(8,128)S(1)}, f32[2,32,256]{2,1,0:T(8,128)S(1)}, u32[]{:S(2)}, u32[]{:S(2)}) collective-permute-start(f32[2,32,256]{2,1,0:T(8,128)S(1)} %get-tuple-element.94.rest_2_), channel_id=1, source_target_pairs={{0,2},{1,3},{2,0},{3,1},{4,6},{5,7},{6,4},{7,5},{8,10},{9,11},{10,... | collective-permute-start | bytes 196616 | tf_op jit(solution)/shard_map/ppermute | solution.py:328
  110.4 1.7 collective-permute-start.44
  112.1 2.7 %collective-permute-done.42.rest_3_ = f32[6,16,256]{2,1,0:T(8,128)S(1)} collective-permute-done((f32[6,16,256]{2,1,0:T(8,128)S(1)}, f32[6,16,256]{2,1,0:T(8,128)S(1)}, u32[]{:S(2)}, u32[]{:S(2)}) %collective-permute-start.42) | collective-permute-done | bytes 98336 | tf_op jit(solution)/shard_map/ppermute | solution.py:328
  114.9 2.7 %collective-permute-start.43 = (f32[6,16,256]{2,1,0:T(8,128)S(1)}, f32[6,16,256]{2,1,0:T(8,128)S(1)}, u32[]{:S(2)}, u32[]{:S(2)}) collective-permute-start(f32[6,16,256]{2,1,0:T(8,128)S(1)} %collective-permute-done.42.rest_3_), channel_id=1, source_target_pairs={{0,1},{1,0},{2,3},{3,2},{4,5},{5,4},{6,7},{7,6},{8,9},{9,8},{10,11... | collective-permute-start | bytes 294920 | tf_op jit(solution)/shard_map/ppermute | solution.py:328
  119.7 1.7 collective-permute-start.41
  123.6 1.8 shard_map.78.rest_4_
  129.4 2.2 %collective-permute-start.49 = (f32[2,32,256]{2,1,0:T(8,128)S(1)}, f32[2,32,256]{2,1,0:T(8,128)S(1)}, u32[]{:S(2)}, u32[]{:S(2)}) collective-permute-start(f32[2,32,256]{2,1,0:T(8,128)S(1)} %get-tuple-element.104), channel_id=1, source_target_pairs={{0,24},{4,28},{8,16},{12,20},{16,8},{20,12},{24,0},{28,4},{1,25},{... | collective-permute-start | bytes 196616 | tf_op jit(solution)/shard_map/ppermute | solution.py:308
  143.0 2.2 %collective-permute-done.57.rest_2_ = f32[2,32,256]{2,1,0:T(8,128)S(1)} collective-permute-done((f32[2,32,256]{2,1,0:T(8,128)S(1)}, f32[2,32,256]{2,1,0:T(8,128)S(1)}, u32[]{:S(2)}, u32[]{:S(2)}) %collective-permute-start.57) | collective-permute-done | bytes 65568 | tf_op jit(solution)/shard_map/ppermute | solution.py:308
  145.3 2.2 %collective-permute-start.64 = (f32[6,32,256]{2,1,0:T(8,128)S(1)}, f32[6,32,256]{2,1,0:T(8,128)S(1)}, u32[]{:S(2)}, u32[]{:S(2)}) collective-permute-start(f32[6,32,256]{2,1,0:T(8,128)S(1)} %get-tuple-element.111.rest_3_), channel_id=1, source_target_pairs={{0,1},{1,0},{2,3},{3,2},{4,5},{5,4},{6,7},{7,6},{8,9},{9,8},{10,11... | collective-permute-start | bytes 589832 | tf_op jit(solution)/shard_map/ppermute | solution.py:328
  147.9 2.5 %collective-permute-start.54 = (f32[2,32,256]{2,1,0:T(8,128)S(1)}, f32[2,32,256]{2,1,0:T(8,128)S(1)}, u32[]{:S(2)}, u32[]{:S(2)}) collective-permute-start(f32[2,32,256]{2,1,0:T(8,128)S(1)} %get-tuple-element.105.rest_2_), channel_id=1, source_target_pairs={{0,2},{1,3},{2,0},{3,1},{4,6},{5,7},{6,4},{7,5},{8,10},{9,11},{10,... | collective-permute-start | bytes 196616 | tf_op jit(solution)/shard_map/ppermute | solution.py:328
  150.4 1.8 %collective-permute-start.62 = (f32[6,16,256]{2,1,0:T(8,128)S(1)}, f32[6,16,256]{2,1,0:T(8,128)S(1)}, u32[]{:S(2)}, u32[]{:S(2)}) collective-permute-start(f32[6,16,256]{2,1,0:T(8,128)S(1)} %get-tuple-element.109), channel_id=1, source_target_pairs={{0,3},{1,2},{2,1},{3,0},{4,7},{5,6},{6,5},{7,4},{8,11},{9,10},{10,... | collective-permute-start | bytes 294920 | tf_op jit(solution)/shard_map/ppermute | solution.py:328
  152.2 2.6 %collective-permute-done.60.rest_3_ = f32[6,16,256]{2,1,0:T(8,128)S(1)} collective-permute-done((f32[6,16,256]{2,1,0:T(8,128)S(1)}, f32[6,16,256]{2,1,0:T(8,128)S(1)}, u32[]{:S(2)}, u32[]{:S(2)}) %collective-permute-start.60) | collective-permute-done | bytes 98336 | tf_op jit(solution)/shard_map/ppermute | solution.py:328
  154.9 2.8 %collective-permute-start.61 = (f32[6,16,256]{2,1,0:T(8,128)S(1)}, f32[6,16,256]{2,1,0:T(8,128)S(1)}, u32[]{:S(2)}, u32[]{:S(2)}) collective-permute-start(f32[6,16,256]{2,1,0:T(8,128)S(1)} %collective-permute-done.60.rest_3_), channel_id=1, source_target_pairs={{0,1},{1,0},{2,3},{3,2},{4,5},{5,4},{6,7},{7,6},{8,9},{9,8},{10,11... | collective-permute-start | bytes 294920 | tf_op jit(solution)/shard_map/ppermute | solution.py:328
  159.7 1.8 %collective-permute-start.59 = (f32[2,32,256]{2,1,0:T(8,128)S(1)}, f32[2,32,256]{2,1,0:T(8,128)S(1)}, u32[]{:S(2)}, u32[]{:S(2)}) collective-permute-start(f32[2,32,256]{2,1,0:T(8,128)S(1)} %get-tuple-element.105.rest_2_), channel_id=1, source_target_pairs={{0,3},{1,2},{2,1},{3,0},{4,7},{5,6},{6,5},{7,4},{8,11},{9,10},{10,... | collective-permute-start | bytes 196616 | tf_op jit(solution)/shard_map/ppermute | solution.py:328
  169.5 2.1 %collective-permute-start.67 = (f32[2,32,256]{2,1,0:T(8,128)S(1)}, f32[2,32,256]{2,1,0:T(8,128)S(1)}, u32[]{:S(2)}, u32[]{:S(2)}) collective-permute-start(f32[2,32,256]{2,1,0:T(8,128)S(1)} %get-tuple-element.115), channel_id=1, source_target_pairs={{0,24},{4,28},{8,16},{12,20},{16,8},{20,12},{24,0},{28,4},{1,25},{... | collective-permute-start | bytes 196616 | tf_op jit(solution)/shard_map/ppermute | solution.py:308
  172.9 1.7 collective-permute-done.67.rest_3_
  (147 shorter events, 87.6 us)
Async XLA Ops:
  4.8 5.3 %collective-permute-start.2 = (f32[2,32,256]{2,1,0:T(8,128)S(1)}, f32[2,32,256]{2,1,0:T(8,128)S(1)}, u32[]{:S(2)}, u32[]{:S(2)}) collective-permute-start(f32[2,32,256]{2,1,0:T(8,128)S(1)} %get-tuple-element.67.rest_9_), channel_id=1, source_target_pairs={{0,8},{4,12},{8,0},{12,4},{16,24},{20,28},{24,16},{28,20},{1,9},{5... | collective-permute-start | bytes 196616 | tf_op jit(solution)/shard_map/ppermute | solution.py:308
  9.0 5.2 %collective-permute-start.4 = (f32[2,32,256]{2,1,0:T(8,128)S(1)}, f32[2,32,256]{2,1,0:T(8,128)S(1)}, u32[]{:S(2)}, u32[]{:S(2)}) collective-permute-start(f32[2,32,256]{2,1,0:T(8,128)S(1)} %get-tuple-element.69.rest_11_), channel_id=1, source_target_pairs={{0,24},{4,28},{8,16},{12,20},{16,8},{20,12},{24,0},{28,4},{1,25},{... | collective-permute-start | bytes 196616 | tf_op jit(solution)/shard_map/ppermute | solution.py:308
  14.2 29.7 %collective-permute-start.10 = (f32[6,32,256]{2,1,0:T(8,128)S(1)}, f32[6,32,256]{2,1,0:T(8,128)S(1)}, u32[]{:S(2)}, u32[]{:S(2)}) collective-permute-start(f32[6,32,256]{2,1,0:T(8,128)S(1)} %shard_map.61.rest_1_), channel_id=1, source_target_pairs={{0,1},{1,0},{2,3},{3,2},{4,5},{5,4},{6,7},{7,6},{8,9},{9,8},{10,11... | collective-permute-start | bytes 589832 | tf_op jit(solution)/shard_map/ppermute | solution.py:328
  15.9 29.6 %collective-permute-start.8 = (f32[6,32,256]{2,1,0:T(8,128)S(1)}, f32[6,32,256]{2,1,0:T(8,128)S(1)}, u32[]{:S(2)}, u32[]{:S(2)}) collective-permute-start(f32[6,32,256]{2,1,0:T(8,128)S(1)} %shard_map.61.rest_1_), channel_id=1, source_target_pairs={{0,2},{1,3},{2,0},{3,1},{4,6},{5,7},{6,4},{7,5},{8,10},{9,11},{10,... | collective-permute-start | bytes 589832 | tf_op jit(solution)/shard_map/ppermute | solution.py:328
  18.4 28.6 %collective-permute-start.6 = (f32[6,32,256]{2,1,0:T(8,128)S(1)}, f32[6,32,256]{2,1,0:T(8,128)S(1)}, u32[]{:S(2)}, u32[]{:S(2)}) collective-permute-start(f32[6,32,256]{2,1,0:T(8,128)S(1)} %shard_map.61.rest_1_), channel_id=1, source_target_pairs={{0,3},{1,2},{2,1},{3,0},{4,7},{5,6},{6,5},{7,4},{8,11},{9,10},{10,... | collective-permute-start | bytes 589832 | tf_op jit(solution)/shard_map/ppermute | solution.py:328
  18.7 11.4 %collective-permute-start.9 = (f32[2,32,256]{2,1,0:T(8,128)S(1)}, f32[2,32,256]{2,1,0:T(8,128)S(1)}, u32[]{:S(2)}, u32[]{:S(2)}) collective-permute-start(f32[2,32,256]{2,1,0:T(8,128)S(1)} %get-tuple-element.66.rest_0_.rest_8_), channel_id=1, source_target_pairs={{0,1},{1,0},{2,3},{3,2},{4,5},{5,4},{6,7},{7,6},{8,9},{9,8},{10,11... | collective-permute-start | bytes 196616 | tf_op jit(solution)/shard_map/ppermute | solution.py:328
  19.3 26.1 %collective-permute-start.7 = (f32[2,32,256]{2,1,0:T(8,128)S(1)}, f32[2,32,256]{2,1,0:T(8,128)S(1)}, u32[]{:S(2)}, u32[]{:S(2)}) collective-permute-start(f32[2,32,256]{2,1,0:T(8,128)S(1)} %get-tuple-element.66.rest_0_.rest_8_), channel_id=1, source_target_pairs={{0,2},{1,3},{2,0},{3,1},{4,6},{5,7},{6,4},{7,5},{8,10},{9,11},{10,... | collective-permute-start | bytes 196616 | tf_op jit(solution)/shard_map/ppermute | solution.py:328
  30.1 16.9 %collective-permute-start.5 = (f32[2,32,256]{2,1,0:T(8,128)S(1)}, f32[2,32,256]{2,1,0:T(8,128)S(1)}, u32[]{:S(2)}, u32[]{:S(2)}) collective-permute-start(f32[2,32,256]{2,1,0:T(8,128)S(1)} %get-tuple-element.66.rest_0_.rest_8_), channel_id=1, source_target_pairs={{0,3},{1,2},{2,1},{3,0},{4,7},{5,6},{6,5},{7,4},{8,11},{9,10},{10,... | collective-permute-start | bytes 196616 | tf_op jit(solution)/shard_map/ppermute | solution.py:328
  65.8 17.5 %collective-permute-start.28 = (f32[6,32,256]{2,1,0:T(8,128)S(1)}, f32[6,32,256]{2,1,0:T(8,128)S(1)}, u32[]{:S(2)}, u32[]{:S(2)}) collective-permute-start(f32[6,32,256]{2,1,0:T(8,128)S(1)} %get-tuple-element.87.rest_3_), channel_id=1, source_target_pairs={{0,1},{1,0},{2,3},{3,2},{4,5},{5,4},{6,7},{7,6},{8,9},{9,8},{10,11... | collective-permute-start | bytes 589832 | tf_op jit(solution)/shard_map/ppermute | solution.py:328
  67.5 7.4 %collective-permute-start.24 = (f32[6,16,256]{2,1,0:T(8,128)S(1)}, f32[6,16,256]{2,1,0:T(8,128)S(1)}, u32[]{:S(2)}, u32[]{:S(2)}) collective-permute-start(f32[6,16,256]{2,1,0:T(8,128)S(1)} %get-tuple-element.86), channel_id=1, source_target_pairs={{0,2},{1,3},{2,0},{3,1},{4,6},{5,7},{6,4},{7,5},{8,10},{9,11},{10,... | collective-permute-start | bytes 294920 | tf_op jit(solution)/shard_map/ppermute | solution.py:328
  67.8 11.1 %collective-permute-start.18 = (f32[2,32,256]{2,1,0:T(8,128)S(1)}, f32[2,32,256]{2,1,0:T(8,128)S(1)}, u32[]{:S(2)}, u32[]{:S(2)}) collective-permute-start(f32[2,32,256]{2,1,0:T(8,128)S(1)} %get-tuple-element.81.rest_2_), channel_id=1, source_target_pairs={{0,2},{1,3},{2,0},{3,1},{4,6},{5,7},{6,4},{7,5},{8,10},{9,11},{10,... | collective-permute-start | bytes 196616 | tf_op jit(solution)/shard_map/ppermute | solution.py:328
  70.4 9.3 %collective-permute-start.27 = (f32[2,32,256]{2,1,0:T(8,128)S(1)}, f32[2,32,256]{2,1,0:T(8,128)S(1)}, u32[]{:S(2)}, u32[]{:S(2)}) collective-permute-start(f32[2,32,256]{2,1,0:T(8,128)S(1)} %get-tuple-element.81.rest_2_), channel_id=1, source_target_pairs={{0,1},{1,0},{2,3},{3,2},{4,5},{5,4},{6,7},{7,6},{8,9},{9,8},{10,11... | collective-permute-start | bytes 196616 | tf_op jit(solution)/shard_map/ppermute | solution.py:328
  70.8 15.0 %collective-permute-start.26 = (f32[6,16,256]{2,1,0:T(8,128)S(1)}, f32[6,16,256]{2,1,0:T(8,128)S(1)}, u32[]{:S(2)}, u32[]{:S(2)}) collective-permute-start(f32[6,16,256]{2,1,0:T(8,128)S(1)} %get-tuple-element.85), channel_id=1, source_target_pairs={{0,3},{1,2},{2,1},{3,0},{4,7},{5,6},{6,5},{7,4},{8,11},{9,10},{10,... | collective-permute-start | bytes 294920 | tf_op jit(solution)/shard_map/ppermute | solution.py:328
  74.9 11.7 %collective-permute-start.25 = (f32[6,16,256]{2,1,0:T(8,128)S(1)}, f32[6,16,256]{2,1,0:T(8,128)S(1)}, u32[]{:S(2)}, u32[]{:S(2)}) collective-permute-start(f32[6,16,256]{2,1,0:T(8,128)S(1)} %collective-permute-done.24.rest_3_), channel_id=1, source_target_pairs={{0,1},{1,0},{2,3},{3,2},{4,5},{5,4},{6,7},{7,6},{8,9},{9,8},{10,11... | collective-permute-start | bytes 294920 | tf_op jit(solution)/shard_map/ppermute | solution.py:328
  78.9 8.4 %collective-permute-start.22 = (f32[6,16,256]{2,1,0:T(8,128)S(1)}, f32[6,16,256]{2,1,0:T(8,128)S(1)}, u32[]{:S(2)}, u32[]{:S(2)}) collective-permute-start(f32[6,16,256]{2,1,0:T(8,128)S(1)} %get-tuple-element.85), channel_id=1, source_target_pairs={{0,2},{1,3},{2,0},{3,1},{4,6},{5,7},{6,4},{7,5},{8,10},{9,11},{10,... | collective-permute-start | bytes 294920 | tf_op jit(solution)/shard_map/ppermute | solution.py:328
  79.7 6.2 %collective-permute-start.23 = (f32[2,32,256]{2,1,0:T(8,128)S(1)}, f32[2,32,256]{2,1,0:T(8,128)S(1)}, u32[]{:S(2)}, u32[]{:S(2)}) collective-permute-start(f32[2,32,256]{2,1,0:T(8,128)S(1)} %get-tuple-element.81.rest_2_), channel_id=1, source_target_pairs={{0,3},{1,2},{2,1},{3,0},{4,7},{5,6},{6,5},{7,4},{8,11},{9,10},{10,... | collective-permute-start | bytes 196616 | tf_op jit(solution)/shard_map/ppermute | solution.py:328
  105.3 18.3 %collective-permute-start.46 = (f32[6,32,256]{2,1,0:T(8,128)S(1)}, f32[6,32,256]{2,1,0:T(8,128)S(1)}, u32[]{:S(2)}, u32[]{:S(2)}) collective-permute-start(f32[6,32,256]{2,1,0:T(8,128)S(1)} %get-tuple-element.100.rest_3_), channel_id=1, source_target_pairs={{0,1},{1,0},{2,3},{3,2},{4,5},{5,4},{6,7},{7,6},{8,9},{9,8},{10,11... | collective-permute-start | bytes 589832 | tf_op jit(solution)/shard_map/ppermute | solution.py:328
  107.4 7.4 %collective-permute-start.42 = (f32[6,16,256]{2,1,0:T(8,128)S(1)}, f32[6,16,256]{2,1,0:T(8,128)S(1)}, u32[]{:S(2)}, u32[]{:S(2)}) collective-permute-start(f32[6,16,256]{2,1,0:T(8,128)S(1)} %get-tuple-element.99), channel_id=1, source_target_pairs={{0,2},{1,3},{2,0},{3,1},{4,6},{5,7},{6,4},{7,5},{8,10},{9,11},{10,... | collective-permute-start | bytes 294920 | tf_op jit(solution)/shard_map/ppermute | solution.py:328
  107.7 11.1 %collective-permute-start.36 = (f32[2,32,256]{2,1,0:T(8,128)S(1)}, f32[2,32,256]{2,1,0:T(8,128)S(1)}, u32[]{:S(2)}, u32[]{:S(2)}) collective-permute-start(f32[2,32,256]{2,1,0:T(8,128)S(1)} %get-tuple-element.94.rest_2_), channel_id=1, source_target_pairs={{0,2},{1,3},{2,0},{3,1},{4,6},{5,7},{6,4},{7,5},{8,10},{9,11},{10,... | collective-permute-start | bytes 196616 | tf_op jit(solution)/shard_map/ppermute | solution.py:328
  110.4 9.3 %collective-permute-start.45 = (f32[2,32,256]{2,1,0:T(8,128)S(1)}, f32[2,32,256]{2,1,0:T(8,128)S(1)}, u32[]{:S(2)}, u32[]{:S(2)}) collective-permute-start(f32[2,32,256]{2,1,0:T(8,128)S(1)} %get-tuple-element.94.rest_2_), channel_id=1, source_target_pairs={{0,1},{1,0},{2,3},{3,2},{4,5},{5,4},{6,7},{7,6},{8,9},{9,8},{10,11... | collective-permute-start | bytes 196616 | tf_op jit(solution)/shard_map/ppermute | solution.py:328
  110.4 15.4 %collective-permute-start.44 = (f32[6,16,256]{2,1,0:T(8,128)S(1)}, f32[6,16,256]{2,1,0:T(8,128)S(1)}, u32[]{:S(2)}, u32[]{:S(2)}) collective-permute-start(f32[6,16,256]{2,1,0:T(8,128)S(1)} %get-tuple-element.98), channel_id=1, source_target_pairs={{0,3},{1,2},{2,1},{3,0},{4,7},{5,6},{6,5},{7,4},{8,11},{9,10},{10,... | collective-permute-start | bytes 294920 | tf_op jit(solution)/shard_map/ppermute | solution.py:328
  114.9 11.7 %collective-permute-start.43 = (f32[6,16,256]{2,1,0:T(8,128)S(1)}, f32[6,16,256]{2,1,0:T(8,128)S(1)}, u32[]{:S(2)}, u32[]{:S(2)}) collective-permute-start(f32[6,16,256]{2,1,0:T(8,128)S(1)} %collective-permute-done.42.rest_3_), channel_id=1, source_target_pairs={{0,1},{1,0},{2,3},{3,2},{4,5},{5,4},{6,7},{7,6},{8,9},{9,8},{10,11... | collective-permute-start | bytes 294920 | tf_op jit(solution)/shard_map/ppermute | solution.py:328
  118.8 8.5 %collective-permute-start.40 = (f32[6,16,256]{2,1,0:T(8,128)S(1)}, f32[6,16,256]{2,1,0:T(8,128)S(1)}, u32[]{:S(2)}, u32[]{:S(2)}) collective-permute-start(f32[6,16,256]{2,1,0:T(8,128)S(1)} %get-tuple-element.98), channel_id=1, source_target_pairs={{0,2},{1,3},{2,0},{3,1},{4,6},{5,7},{6,4},{7,5},{8,10},{9,11},{10,... | collective-permute-start | bytes 294920 | tf_op jit(solution)/shard_map/ppermute | solution.py:328
  119.7 6.2 %collective-permute-start.41 = (f32[2,32,256]{2,1,0:T(8,128)S(1)}, f32[2,32,256]{2,1,0:T(8,128)S(1)}, u32[]{:S(2)}, u32[]{:S(2)}) collective-permute-start(f32[2,32,256]{2,1,0:T(8,128)S(1)} %get-tuple-element.94.rest_2_), channel_id=1, source_target_pairs={{0,3},{1,2},{2,1},{3,0},{4,7},{5,6},{6,5},{7,4},{8,11},{9,10},{10,... | collective-permute-start | bytes 196616 | tf_op jit(solution)/shard_map/ppermute | solution.py:328
  145.3 18.5 %collective-permute-start.64 = (f32[6,32,256]{2,1,0:T(8,128)S(1)}, f32[6,32,256]{2,1,0:T(8,128)S(1)}, u32[]{:S(2)}, u32[]{:S(2)}) collective-permute-start(f32[6,32,256]{2,1,0:T(8,128)S(1)} %get-tuple-element.111.rest_3_), channel_id=1, source_target_pairs={{0,1},{1,0},{2,3},{3,2},{4,5},{5,4},{6,7},{7,6},{8,9},{9,8},{10,11... | collective-permute-start | bytes 589832 | tf_op jit(solution)/shard_map/ppermute | solution.py:328
  147.4 7.4 %collective-permute-start.60 = (f32[6,16,256]{2,1,0:T(8,128)S(1)}, f32[6,16,256]{2,1,0:T(8,128)S(1)}, u32[]{:S(2)}, u32[]{:S(2)}) collective-permute-start(f32[6,16,256]{2,1,0:T(8,128)S(1)} %get-tuple-element.110), channel_id=1, source_target_pairs={{0,2},{1,3},{2,0},{3,1},{4,6},{5,7},{6,4},{7,5},{8,10},{9,11},{10,... | collective-permute-start | bytes 294920 | tf_op jit(solution)/shard_map/ppermute | solution.py:328
  147.9 10.9 %collective-permute-start.54 = (f32[2,32,256]{2,1,0:T(8,128)S(1)}, f32[2,32,256]{2,1,0:T(8,128)S(1)}, u32[]{:S(2)}, u32[]{:S(2)}) collective-permute-start(f32[2,32,256]{2,1,0:T(8,128)S(1)} %get-tuple-element.105.rest_2_), channel_id=1, source_target_pairs={{0,2},{1,3},{2,0},{3,1},{4,6},{5,7},{6,4},{7,5},{8,10},{9,11},{10,... | collective-permute-start | bytes 196616 | tf_op jit(solution)/shard_map/ppermute | solution.py:328
  150.4 9.3 %collective-permute-start.63 = (f32[2,32,256]{2,1,0:T(8,128)S(1)}, f32[2,32,256]{2,1,0:T(8,128)S(1)}, u32[]{:S(2)}, u32[]{:S(2)}) collective-permute-start(f32[2,32,256]{2,1,0:T(8,128)S(1)} %get-tuple-element.105.rest_2_), channel_id=1, source_target_pairs={{0,1},{1,0},{2,3},{3,2},{4,5},{5,4},{6,7},{7,6},{8,9},{9,8},{10,11... | collective-permute-start | bytes 196616 | tf_op jit(solution)/shard_map/ppermute | solution.py:328
  150.4 15.3 %collective-permute-start.62 = (f32[6,16,256]{2,1,0:T(8,128)S(1)}, f32[6,16,256]{2,1,0:T(8,128)S(1)}, u32[]{:S(2)}, u32[]{:S(2)}) collective-permute-start(f32[6,16,256]{2,1,0:T(8,128)S(1)} %get-tuple-element.109), channel_id=1, source_target_pairs={{0,3},{1,2},{2,1},{3,0},{4,7},{5,6},{6,5},{7,4},{8,11},{9,10},{10,... | collective-permute-start | bytes 294920 | tf_op jit(solution)/shard_map/ppermute | solution.py:328
  154.9 11.6 %collective-permute-start.61 = (f32[6,16,256]{2,1,0:T(8,128)S(1)}, f32[6,16,256]{2,1,0:T(8,128)S(1)}, u32[]{:S(2)}, u32[]{:S(2)}) collective-permute-start(f32[6,16,256]{2,1,0:T(8,128)S(1)} %collective-permute-done.60.rest_3_), channel_id=1, source_target_pairs={{0,1},{1,0},{2,3},{3,2},{4,5},{5,4},{6,7},{7,6},{8,9},{9,8},{10,11... | collective-permute-start | bytes 294920 | tf_op jit(solution)/shard_map/ppermute | solution.py:328
  158.7 8.5 %collective-permute-start.58 = (f32[6,16,256]{2,1,0:T(8,128)S(1)}, f32[6,16,256]{2,1,0:T(8,128)S(1)}, u32[]{:S(2)}, u32[]{:S(2)}) collective-permute-start(f32[6,16,256]{2,1,0:T(8,128)S(1)} %get-tuple-element.109), channel_id=1, source_target_pairs={{0,2},{1,3},{2,0},{3,1},{4,6},{5,7},{6,4},{7,5},{8,10},{9,11},{10,... | collective-permute-start | bytes 294920 | tf_op jit(solution)/shard_map/ppermute | solution.py:328
  159.7 6.1 %collective-permute-start.59 = (f32[2,32,256]{2,1,0:T(8,128)S(1)}, f32[2,32,256]{2,1,0:T(8,128)S(1)}, u32[]{:S(2)}, u32[]{:S(2)}) collective-permute-start(f32[2,32,256]{2,1,0:T(8,128)S(1)} %get-tuple-element.105.rest_2_), channel_id=1, source_target_pairs={{0,3},{1,2},{2,1},{3,0},{4,7},{5,6},{6,5},{7,4},{8,11},{9,10},{10,... | collective-permute-start | bytes 196616 | tf_op jit(solution)/shard_map/ppermute | solution.py:328
  (41 other events, 148.4 us)
where the time goes:
time: 177 us
  starting transfers between devices  76.5 us (43%)
  waiting for transfers between devices  56.6 us (32%)
  Pallas kernels  43.2 us (24%)
    ppermute x30, starting transfers between devices, shift(): return lax.ppermute(x, 'rcv', [(i, i ^ d) for i in range(z_size)])  46.7 us
    ppermute x42, waiting for transfers between devices, trade(): return lax.ppermute(x, 'freq', [(i, i ^ d) for i in range(n_f)])  35.4 us
    pallas_call x32, Pallas kernels, call(): pl.pallas_call(body, in_specs=ins, out_specs=tuple((VMEM for _ in outs)),...  31.8 us
    ppermute x42, starting transfers between devices, trade(): return lax.ppermute(x, 'freq', [(i, i ^ d) for i in range(n_f)])  29.8 us
    ppermute x30, waiting for transfers between devices, shift(): return lax.ppermute(x, 'rcv', [(i, i ^ d) for i in range(z_size)])  21.2 us
    pallas_call x1, Pallas kernels, hold(): pl.pallas_call(functools.partial(hold_body, z_size, parity, len(arrays)),...  11.4 us
  transfers between devices with their start and end apart: 72, of which 38 were waited for; matrix products, arithmetic and copies ran while one was open for 0% of the time, Pallas kernels for 18%

commit v1 on v0

--- a/solution.py
+++ b/solution.py
@@ -58,8 +58,8 @@
     return series * x
 
 
-def make_table(order, me, n, th, tl, scale):
-    rows, samples = th.shape
+def make_table(order, me, n, samples, scale):
+    rows = scale.shape[0]
     shape = (rows, samples)
     time = lax.broadcasted_iota(jnp.int32, shape, 1).astype(F32) / samples
     part = (lax.broadcasted_iota(jnp.int32, shape, 0) & 1).astype(F32) * 0.25
@@ -70,62 +70,66 @@
     q = column(order, rows, slot)
     scale[...] = jnp.where(q == 0.0, 1.0, 2.0) / samples
     turn = q * time + part
-    table = halves(cosine(turn - jnp.floor(turn)))
-    th[...] = table[0]
-    tl[...] = table[1]
-    return table
-
-
-def spectrum_body(n, order_in, onset_in, x_in, me, th, tl, scale, limit, *rest):
-    *outs, order, onset, x, sems = rest
+    return cosine(turn - jnp.floor(turn))
+
+
+def spectrum_body(n, order_in, onset_in, x_in, th, tl, scale, limit, out, order, onset, x, sems):
     pairs = ((order_in, order), (onset_in, onset), (x_in, x))
     copies = [pltpu.make_async_copy(a, b, sems.at[i]) for i, (a, b) in enumerate(pairs)]
     for copy in copies:
         copy.start()
     copies[0].wait()
-    table = make_table(order[...], me[0], n, th, tl, scale)
+    table = halves(make_table(order[...], 0, n, x.shape[1], scale))
+    th[...] = table[0]
+    tl[...] = table[1]
     copies[1].wait()
     limit[...] = column(onset[...], limit.shape[0], lambda r: r).astype(jnp.int32)
     copies[2].wait()
-    y = dot3(table, halves(x[...]), 1, 1)
-    if len(outs) == 1:
-        outs[0][...] = y
-        return
+    out[...] = dot3(table, halves(x[...]), 1, 1)
+
+
+def pair_table_body(chips, n, order_in, onset_in, x_in, me, mh, ml, bh, bl, scale, *rest):
+    onset, x, order, sems = rest
+    pairs = ((order_in, order), (onset_in, onset), (x_in, x))
+    copies = [pltpu.make_async_copy(a, b, sems.at[i]) for i, (a, b) in enumerate(pairs)]
+    for copy in copies:
+        copy.start()
+    copies[0].wait()
+    table = make_table(order[...], me[0], n, x.shape[1], scale)
     step = 2 * n
-    for j in range(y.shape[0] // step):
-        outs[j % 2][j // 2] = y[j * step : (j + 1) * step]
-
-
-def pair_body(keep, given, limit, onset, both, *outs):
-    both[0] = limit[...]
-    both[1] = column(onset[...], limit.shape[0], lambda r: r).astype(jnp.int32)
+    mine = [table[2 * q * step : (2 * q + 1) * step] for q in range(chips)]
+    mh[...], ml[...] = halves(jnp.concatenate(mine, axis=0))
+    bh[...], bl[...] = halves(table.T)
+    copies[1].wait()
+    copies[2].wait()
+
+
+def pair_spectrum_body(mh, ml, own, other, onset, other_onset, limit, *outs):
+    step, width = outs[0].shape[1:]
+    y = jnp.concatenate([own[...], other[...]], axis=0)
+    z = dot3((mh[...], ml[...]), halves(y), 1, 1)
     for q, out in enumerate(outs):
-        out[0] = keep[q]
-        out[1] = given[q]
-
-
-def pair_mute_body(chips, last, base, scale, onset, th, tl, *rest):
+        for j in range(2):
+            out[j] = z[q * step : (q + 1) * step, j * width : (j + 1) * width]
+    limit[...] = jnp.concatenate([onset[...], other_onset[...]], axis=1)
+
+
+def pair_mute_body(chips, last, base, scale, onset, mh, ml, bh, bl, *rest):
     own, other, rest = rest[:chips], rest[chips : 2 * chips], list(rest[2 * chips :])
     base = [rest.pop(0) for _ in range(base)]
-    points = 1 if last else 2
-    step = own[0].shape[1]
+    step, width = own[0].shape[1:]
     fields = []
-    for j in range(points):
+    for j in range(1 if last else 2):
         parts = [x[i] for q in range(chips) for x, i in ((own[q], j), (other[q], 1 - j))]
-        fields.append((jnp.concatenate(parts, axis=0) * scale[...]).T)
-    y = dot3(halves(jnp.concatenate(fields, axis=0)), (th[...], tl[...]), 1, 0)
-    t = lax.broadcasted_iota(jnp.int32, y.shape, 1)
-    limit = jnp.concatenate([onset[j] for j in range(points)], axis=0)
-    y = jnp.where(t < limit, y, 0.0)
+        fields.append(jnp.concatenate(parts, axis=0))
+    fields = jnp.concatenate(fields, axis=1) * scale[...]
+    y = dot3((bh[...], bl[...]), halves(fields), 1, 0)
+    t = lax.broadcasted_iota(jnp.int32, y.shape, 0)
+    y = jnp.where(t < onset[:, : y.shape[1]], y, 0.0)
     if last:
-        rest[0][...] = base[0][...] + y if base else y
+        rest[0][...] = base[0][...] + y.T if base else y.T
         return
-    mine = [
-        jnp.concatenate([x[2 * q * step : (2 * q + 1) * step, :] for q in range(chips)], axis=0)
-        for x in (th, tl)
-    ]
-    z = dot3(mine, halves(y), 1, 1)
-    width = z.shape[1] // 2
+    z = dot3((mh[...], ml[...]), halves(y), 1, 0)
     for q, out in enumerate(rest):
         for j in range(2):
             piece = z[q * step : (q + 1) * step, j * width : (j + 1) * width]
@@ -276,33 +280,11 @@
     points = n_f * own
     chips = 4 if n_f == 8 and own == 1 and n % 2 == 0 and z_size == 4 else 0
     place = lax.axis_index("rcv")[None].astype(jnp.int32)
-    me = lax.axis_index("freq")[None].astype(jnp.int32) * (1 if chips else 0)
+    me = lax.axis_index("freq")[None].astype(jnp.int32)
     smem = pl.BlockSpec(memory_space=pltpu.SMEM)
 
     n_rows = 2 * freq_order.shape[0]
     traces = focus_start.reshape(own * rows, samples)
-    if chips:
-        spectra = [sds((chips, 2 * n, rows), F32)] * 2
-    else:
-        spectra = [sds((n_rows, own * rows), F32)]
-    th, tl, scale, limit, *start = call(
-        functools.partial(spectrum_body, n),
-        [HBM] * 3 + [smem],
-        [sds((n_rows, samples), BF16)] * 2
-        + [sds((n_rows, 1), F32), sds((own * rows, 1), jnp.int32)]
-        + spectra,
-        [
-            pltpu.with_memory_space_constraint(x, pltpu.HBM)
-            for x in (freq_order.reshape(1, -1), onset.reshape(1, -1), traces)
-        ]
-        + [me],
-        scratch=[
-            pltpu.VMEM((1, n_rows // 2), jnp.int32),
-            pltpu.VMEM((1, own * rows), jnp.int32),
-            pltpu.VMEM((own * rows, samples), F32),
-            pltpu.SemaphoreType.DMA((3,)),
-        ],
-    )
 
     def trade(x, d):
         return lax.ppermute(x, "freq", [(i, i ^ d) for i in range(n_f)])
@@ -311,16 +293,44 @@
         moved = {q: trade(pieces[q], 2 * q) for q in (3, 1, 2)}
         return [pieces[0]] + [moved[q] for q in (1, 2, 3)]
 
+    def from_hbm(*arrays):
+        return [pltpu.with_memory_space_constraint(x, pltpu.HBM) for x in arrays]
+
+    order, limit = freq_order.reshape(1, -1), onset.reshape(1, -1)
+    order_scratch = pltpu.VMEM((1, n_rows // 2), jnp.int32)
     if chips:
-        given = trade(start[1], 1)
+        given = trade(traces, 1)
+        other = trade(limit, 1)
+        *table, scale, near_limit, local = call(
+            functools.partial(pair_table_body, chips, n),
+            [HBM] * 3 + [smem],
+            [sds((n_rows // 2, samples), BF16)] * 2
+            + [sds((samples, n_rows), BF16)] * 2
+            + [sds((n_rows, 1), F32), sds((1, rows), jnp.int32), sds((rows, samples), F32)],
+            [*from_hbm(order, limit, traces), me],
+            scratch=[order_scratch, pltpu.SemaphoreType.DMA((3,))],
+        )
         limit, *start = call(
-            pair_body,
-            [VMEM] * 4,
-            [sds((2, rows, 1), jnp.int32)] + [sds((2, 2 * n, rows), F32)] * chips,
-            (start[0], given, limit, trade(onset, 1)),
+            pair_spectrum_body,
+            [VMEM] * 6,
+            [sds((1, 2 * rows), jnp.int32)] + [sds((2, 2 * n, rows), F32)] * chips,
+            (*table[:2], local, given, near_limit, other),
         )
     else:
-        start = start[0]
+        *table, scale, limit, start = call(
+            functools.partial(spectrum_body, n),
+            [HBM] * 3,
+            [sds((n_rows, samples), BF16)] * 2
+            + [sds((n_rows, 1), F32), sds((own * rows, 1), jnp.int32)]
+            + [sds((n_rows, own * rows), F32)],
+            from_hbm(order, limit, traces),
+            scratch=[
+                order_scratch,
+                pltpu.VMEM((1, own * rows), jnp.int32),
+                pltpu.VMEM((own * rows, samples), F32),
+                pltpu.SemaphoreType.DMA((3,)),
+            ],
+        )
 
     held = None
 
@@ -414,12 +424,12 @@
         if chips:
             base = [] if base is None else [base] if last else base
             outs = [sds((rows, samples), F32)] if last else [sds((2, 2 * n, rows), F32)] * chips
-            args = (scale, limit, th, tl, *back, *base)
+            args = (scale, limit, *table, *back, *base)
             body = functools.partial(pair_mute_body, chips, last, len(base))
             got = call(body, [VMEM] * len(args), outs, args)
             return got[0] if last else got
         outs = [sds((own * rows, samples) if last else (n_rows, own * rows), F32)]
-        args = (scale, limit, back, th, tl) + (() if base is None else (base,))
+        args = (scale, limit, back, *table) + (() if base is None else (base,))
         body = functools.partial(mute_body, last, base is not None)
         return call(body, [VMEM] * len(args), outs, args)[0]
 

time: 177 us -> 176 us (level)
  waiting for transfers between devices: 56.6 us -> 54.7 us
  transfers between devices with their start and end apart: 72 -> 72, of which waited for: 38 -> 38; matrix products, arithmetic and copies ran while one was open for 0% -> 0% of each run, Pallas kernels for 18% -> 19%
where the time goes in v1:
time: 176 us; the launch traced here: 175 us
  starting transfers between devices  77.5 us (44%)
  waiting for transfers between devices  54.7 us (31%)
  Pallas kernels  42.3 us (24%)
    ppermute x30, starting transfers between devices, shift(): return lax.ppermute(x, 'rcv', [(i, i ^ d) for i in range(z_size)])  47.5 us
    ppermute x42, waiting for transfers between devices, trade(): return lax.ppermute(x, 'freq', [(i, i ^ d) for i in range(n_f)])  34.5 us
    pallas_call x32, Pallas kernels, call(): pl.pallas_call(body, in_specs=ins, out_specs=tuple((VMEM for _ in outs)),...  30.9 us
    ppermute x42, starting transfers between devices, trade(): return lax.ppermute(x, 'freq', [(i, i ^ d) for i in range(n_f)])  30 us
    ppermute x30, waiting for transfers between devices, shift(): return lax.ppermute(x, 'rcv', [(i, i ^ d) for i in range(z_size)])  20.2 us
    pallas_call x1, Pallas kernels, hold(): pl.pallas_call(functools.partial(hold_body, z_size, parity, len(arrays)),...  11.4 us
  transfers between devices with their start and end apart: 72, of which 38 were waited for; matrix products, arithmetic and copies ran while one was open for 0% of the time, Pallas kernels for 19%

profile of v1, /device:TPU:0, one launch (start us, length us, event | category | flops | bytes accessed | tf_op | source)
XLA Modules:
  0.0 175.5 jit_solution(18407859674111262069)
XLA Ops:
  3.6 2.9 %collective-permute-start.2 = (f32[2,32,256]{2,1,0:T(8,128)S(1)}, f32[2,32,256]{2,1,0:T(8,128)S(1)}, u32[]{:S(2)}, u32[]{:S(2)}) collective-permute-start(f32[2,32,256]{2,1,0:T(8,128)S(1)} %get-tuple-element.69.rest_9_), channel_id=1, source_target_pairs={{0,8},{4,12},{8,0},{12,4},{16,24},{20,28},{24,16},{28,20},{1,9},{5... | collective-permute-start | bytes 196616 | tf_op jit(solution)/shard_map/ppermute | solution.py:290
  8.9 1.9 %collective-permute-done.3.rest_1_ = f32[2,32,256]{2,1,0:T(8,128)S(1)} collective-permute-done((f32[2,32,256]{2,1,0:T(8,128)S(1)}, f32[2,32,256]{2,1,0:T(8,128)S(1)}, u32[]{:S(2)}, u32[]{:S(2)}) %collective-permute-start.3) | collective-permute-done | bytes 65568 | tf_op jit(solution)/shard_map/ppermute | solution.py:290
  10.8 2.4 %collective-permute-done.4.rest_2_ = f32[2,32,256]{2,1,0:T(8,128)S(1)} collective-permute-done((f32[2,32,256]{2,1,0:T(8,128)S(1)}, f32[2,32,256]{2,1,0:T(8,128)S(1)}, u32[]{:S(2)}, u32[]{:S(2)}) %collective-permute-start.4) | collective-permute-done | bytes 65568 | tf_op jit(solution)/shard_map/ppermute | solution.py:290
  14.9 2.6 %collective-permute-start.8 = (f32[6,32,256]{2,1,0:T(8,128)S(1)}, f32[6,32,256]{2,1,0:T(8,128)S(1)}, u32[]{:S(2)}, u32[]{:S(2)}) collective-permute-start(f32[6,32,256]{2,1,0:T(8,128)S(1)} %shard_map.61.rest_1_), channel_id=1, source_target_pairs={{0,2},{1,3},{2,0},{3,1},{4,6},{5,7},{6,4},{7,5},{8,10},{9,11},{10,... | collective-permute-start | bytes 589832 | tf_op jit(solution)/shard_map/ppermute | solution.py:338
  18.3 3.5 %collective-permute-start.7 = (f32[2,32,256]{2,1,0:T(8,128)S(1)}, f32[2,32,256]{2,1,0:T(8,128)S(1)}, u32[]{:S(2)}, u32[]{:S(2)}) collective-permute-start(f32[2,32,256]{2,1,0:T(8,128)S(1)} %get-tuple-element.68.rest_0_.rest_8_), channel_id=1, source_target_pairs={{0,2},{1,3},{2,0},{3,1},{4,6},{5,7},{6,4},{7,5},{8,10},{9,11},{10,... | collective-permute-start | bytes 196616 | tf_op jit(solution)/shard_map/ppermute | solution.py:338
  21.8 7.2 %collective-permute-done.9.rest_2_ = f32[2,32,256]{2,1,0:T(8,128)S(1)} collective-permute-done((f32[2,32,256]{2,1,0:T(8,128)S(1)}, f32[2,32,256]{2,1,0:T(8,128)S(1)}, u32[]{:S(2)}, u32[]{:S(2)}) %collective-permute-start.9) | collective-permute-done | bytes 65568 | tf_op jit(solution)/shard_map/ppermute | solution.py:338
  29.1 2.3 %collective-permute-start.5 = (f32[2,32,256]{2,1,0:T(8,128)S(1)}, f32[2,32,256]{2,1,0:T(8,128)S(1)}, u32[]{:S(2)}, u32[]{:S(2)}) collective-permute-start(f32[2,32,256]{2,1,0:T(8,128)S(1)} %get-tuple-element.68.rest_0_.rest_8_), channel_id=1, source_target_pairs={{0,3},{1,2},{2,1},{3,0},{4,7},{5,6},{6,5},{7,4},{8,11},{9,10},{10,... | collective-permute-start | bytes 196616 | tf_op jit(solution)/shard_map/ppermute | solution.py:338
  31.3 11.4 %shard_map.62 = (bf16[2,16,256,256]{3,2,1,0:T(8,128)(2,1)S(1)}, bf16[2,16,256,256]{3,2,1,0:T(8,128)(2,1)S(1)}, bf16[2,16,256,256]{3,2,1,0:T(8,128)(2,1)S(1)}, bf...) custom-call(f32[2,16,256,1024]{3,2,1,0:T(8,128)} %kernel.1, ...), custom_call_target="tpu_custom_call" | custom-call | tf_op jit(solution)/shard_map/pallas_call | solution.py:363
  48.7 2.3 %collective-permute-start.13 = (f32[2,32,256]{2,1,0:T(8,128)S(1)}, f32[2,32,256]{2,1,0:T(8,128)S(1)}, u32[]{:S(2)}, u32[]{:S(2)}) collective-permute-start(f32[2,32,256]{2,1,0:T(8,128)S(1)} %get-tuple-element.82), channel_id=1, source_target_pairs={{0,24},{4,28},{8,16},{12,20},{16,8},{20,12},{24,0},{28,4},{1,25},{... | collective-permute-start | bytes 196616 | tf_op jit(solution)/shard_map/ppermute | solution.py:290
  62.0 2.3 %collective-permute-done.21.rest_2_ = f32[2,32,256]{2,1,0:T(8,128)S(1)} collective-permute-done((f32[2,32,256]{2,1,0:T(8,128)S(1)}, f32[2,32,256]{2,1,0:T(8,128)S(1)}, u32[]{:S(2)}, u32[]{:S(2)}) %collective-permute-start.21) | collective-permute-done | bytes 65568 | tf_op jit(solution)/shard_map/ppermute | solution.py:290
  66.6 2.4 %collective-permute-start.18 = (f32[2,32,256]{2,1,0:T(8,128)S(1)}, f32[2,32,256]{2,1,0:T(8,128)S(1)}, u32[]{:S(2)}, u32[]{:S(2)}) collective-permute-start(f32[2,32,256]{2,1,0:T(8,128)S(1)} %get-tuple-element.83.rest_2_), channel_id=1, source_target_pairs={{0,2},{1,3},{2,0},{3,1},{4,6},{5,7},{6,4},{7,5},{8,10},{9,11},{10,... | collective-permute-start | bytes 196616 | tf_op jit(solution)/shard_map/ppermute | solution.py:338
  71.0 2.5 %collective-permute-done.24.rest_3_ = f32[6,16,256]{2,1,0:T(8,128)S(1)} collective-permute-done((f32[6,16,256]{2,1,0:T(8,128)S(1)}, f32[6,16,256]{2,1,0:T(8,128)S(1)}, u32[]{:S(2)}, u32[]{:S(2)}) %collective-permute-start.24) | collective-permute-done | bytes 98336 | tf_op jit(solution)/shard_map/ppermute | solution.py:338
  73.5 2.6 %collective-permute-start.25 = (f32[6,16,256]{2,1,0:T(8,128)S(1)}, f32[6,16,256]{2,1,0:T(8,128)S(1)}, u32[]{:S(2)}, u32[]{:S(2)}) collective-permute-start(f32[6,16,256]{2,1,0:T(8,128)S(1)} %collective-permute-done.24.rest_3_), channel_id=1, source_target_pairs={{0,1},{1,0},{2,3},{3,2},{4,5},{5,4},{6,7},{7,6},{8,9},{9,8},{10,11... | collective-permute-start | bytes 294920 | tf_op jit(solution)/shard_map/ppermute | solution.py:338
  88.0 2.3 %collective-permute-start.31 = (f32[2,32,256]{2,1,0:T(8,128)S(1)}, f32[2,32,256]{2,1,0:T(8,128)S(1)}, u32[]{:S(2)}, u32[]{:S(2)}) collective-permute-start(f32[2,32,256]{2,1,0:T(8,128)S(1)} %get-tuple-element.95), channel_id=1, source_target_pairs={{0,24},{4,28},{8,16},{12,20},{16,8},{20,12},{24,0},{28,4},{1,25},{... | collective-permute-start | bytes 196616 | tf_op jit(solution)/shard_map/ppermute | solution.py:290
  101.3 2.3 %collective-permute-done.39.rest_2_ = f32[2,32,256]{2,1,0:T(8,128)S(1)} collective-permute-done((f32[2,32,256]{2,1,0:T(8,128)S(1)}, f32[2,32,256]{2,1,0:T(8,128)S(1)}, u32[]{:S(2)}, u32[]{:S(2)}) %collective-permute-start.39) | collective-permute-done | bytes 65568 | tf_op jit(solution)/shard_map/ppermute | solution.py:290
  103.7 2.1 %collective-permute-start.46 = (f32[6,32,256]{2,1,0:T(8,128)S(1)}, f32[6,32,256]{2,1,0:T(8,128)S(1)}, u32[]{:S(2)}, u32[]{:S(2)}) collective-permute-start(f32[6,32,256]{2,1,0:T(8,128)S(1)} %get-tuple-element.102.rest_3_), channel_id=1, source_target_pairs={{0,1},{1,0},{2,3},{3,2},{4,5},{5,4},{6,7},{7,6},{8,9},{9,8},{10,11... | collective-permute-start | bytes 589832 | tf_op jit(solution)/shard_map/ppermute | solution.py:338
  106.2 2.5 %collective-permute-start.36 = (f32[2,32,256]{2,1,0:T(8,128)S(1)}, f32[2,32,256]{2,1,0:T(8,128)S(1)}, u32[]{:S(2)}, u32[]{:S(2)}) collective-permute-start(f32[2,32,256]{2,1,0:T(8,128)S(1)} %get-tuple-element.96.rest_2_), channel_id=1, source_target_pairs={{0,2},{1,3},{2,0},{3,1},{4,6},{5,7},{6,4},{7,5},{8,10},{9,11},{10,... | collective-permute-start | bytes 196616 | tf_op jit(solution)/shard_map/ppermute | solution.py:338
  108.8 1.8 %collective-permute-start.44 = (f32[6,16,256]{2,1,0:T(8,128)S(1)}, f32[6,16,256]{2,1,0:T(8,128)S(1)}, u32[]{:S(2)}, u32[]{:S(2)}) collective-permute-start(f32[6,16,256]{2,1,0:T(8,128)S(1)} %get-tuple-element.100), channel_id=1, source_target_pairs={{0,3},{1,2},{2,1},{3,0},{4,7},{5,6},{6,5},{7,4},{8,11},{9,10},{10,... | collective-permute-start | bytes 294920 | tf_op jit(solution)/shard_map/ppermute | solution.py:338
  110.6 2.7 %collective-permute-done.42.rest_3_ = f32[6,16,256]{2,1,0:T(8,128)S(1)} collective-permute-done((f32[6,16,256]{2,1,0:T(8,128)S(1)}, f32[6,16,256]{2,1,0:T(8,128)S(1)}, u32[]{:S(2)}, u32[]{:S(2)}) %collective-permute-start.42) | collective-permute-done | bytes 98336 | tf_op jit(solution)/shard_map/ppermute | solution.py:338
  113.2 2.8 %collective-permute-start.43 = (f32[6,16,256]{2,1,0:T(8,128)S(1)}, f32[6,16,256]{2,1,0:T(8,128)S(1)}, u32[]{:S(2)}, u32[]{:S(2)}) collective-permute-start(f32[6,16,256]{2,1,0:T(8,128)S(1)} %collective-permute-done.42.rest_3_), channel_id=1, source_target_pairs={{0,1},{1,0},{2,3},{3,2},{4,5},{5,4},{6,7},{7,6},{8,9},{9,8},{10,11... | collective-permute-start | bytes 294920 | tf_op jit(solution)/shard_map/ppermute | solution.py:338
  118.0 1.8 %collective-permute-start.41 = (f32[2,32,256]{2,1,0:T(8,128)S(1)}, f32[2,32,256]{2,1,0:T(8,128)S(1)}, u32[]{:S(2)}, u32[]{:S(2)}) collective-permute-start(f32[2,32,256]{2,1,0:T(8,128)S(1)} %get-tuple-element.96.rest_2_), channel_id=1, source_target_pairs={{0,3},{1,2},{2,1},{3,0},{4,7},{5,6},{6,5},{7,4},{8,11},{9,10},{10,... | collective-permute-start | bytes 196616 | tf_op jit(solution)/shard_map/ppermute | solution.py:338
  122.0 1.7 shard_map.78.rest_4_
  127.7 2.2 %collective-permute-start.49 = (f32[2,32,256]{2,1,0:T(8,128)S(1)}, f32[2,32,256]{2,1,0:T(8,128)S(1)}, u32[]{:S(2)}, u32[]{:S(2)}) collective-permute-start(f32[2,32,256]{2,1,0:T(8,128)S(1)} %get-tuple-element.106), channel_id=1, source_target_pairs={{0,24},{4,28},{8,16},{12,20},{16,8},{20,12},{24,0},{28,4},{1,25},{... | collective-permute-start | bytes 196616 | tf_op jit(solution)/shard_map/ppermute | solution.py:290
  141.0 2.3 %collective-permute-done.57.rest_2_ = f32[2,32,256]{2,1,0:T(8,128)S(1)} collective-permute-done((f32[2,32,256]{2,1,0:T(8,128)S(1)}, f32[2,32,256]{2,1,0:T(8,128)S(1)}, u32[]{:S(2)}, u32[]{:S(2)}) %collective-permute-start.57) | collective-permute-done | bytes 65568 | tf_op jit(solution)/shard_map/ppermute | solution.py:290
  143.4 2.2 %collective-permute-start.64 = (f32[6,32,256]{2,1,0:T(8,128)S(1)}, f32[6,32,256]{2,1,0:T(8,128)S(1)}, u32[]{:S(2)}, u32[]{:S(2)}) collective-permute-start(f32[6,32,256]{2,1,0:T(8,128)S(1)} %get-tuple-element.113.rest_3_), channel_id=1, source_target_pairs={{0,1},{1,0},{2,3},{3,2},{4,5},{5,4},{6,7},{7,6},{8,9},{9,8},{10,11... | collective-permute-start | bytes 589832 | tf_op jit(solution)/shard_map/ppermute | solution.py:338
  146.0 2.5 %collective-permute-start.54 = (f32[2,32,256]{2,1,0:T(8,128)S(1)}, f32[2,32,256]{2,1,0:T(8,128)S(1)}, u32[]{:S(2)}, u32[]{:S(2)}) collective-permute-start(f32[2,32,256]{2,1,0:T(8,128)S(1)} %get-tuple-element.107.rest_2_), channel_id=1, source_target_pairs={{0,2},{1,3},{2,0},{3,1},{4,6},{5,7},{6,4},{7,5},{8,10},{9,11},{10,... | collective-permute-start | bytes 196616 | tf_op jit(solution)/shard_map/ppermute | solution.py:338
  148.6 1.8 %collective-permute-start.62 = (f32[6,16,256]{2,1,0:T(8,128)S(1)}, f32[6,16,256]{2,1,0:T(8,128)S(1)}, u32[]{:S(2)}, u32[]{:S(2)}) collective-permute-start(f32[6,16,256]{2,1,0:T(8,128)S(1)} %get-tuple-element.111), channel_id=1, source_target_pairs={{0,3},{1,2},{2,1},{3,0},{4,7},{5,6},{6,5},{7,4},{8,11},{9,10},{10,... | collective-permute-start | bytes 294920 | tf_op jit(solution)/shard_map/ppermute | solution.py:338
  150.4 2.6 %collective-permute-done.60.rest_3_ = f32[6,16,256]{2,1,0:T(8,128)S(1)} collective-permute-done((f32[6,16,256]{2,1,0:T(8,128)S(1)}, f32[6,16,256]{2,1,0:T(8,128)S(1)}, u32[]{:S(2)}, u32[]{:S(2)}) %collective-permute-start.60) | collective-permute-done | bytes 98336 | tf_op jit(solution)/shard_map/ppermute | solution.py:338
  153.0 2.9 %collective-permute-start.61 = (f32[6,16,256]{2,1,0:T(8,128)S(1)}, f32[6,16,256]{2,1,0:T(8,128)S(1)}, u32[]{:S(2)}, u32[]{:S(2)}) collective-permute-start(f32[6,16,256]{2,1,0:T(8,128)S(1)} %collective-permute-done.60.rest_3_), channel_id=1, source_target_pairs={{0,1},{1,0},{2,3},{3,2},{4,5},{5,4},{6,7},{7,6},{8,9},{9,8},{10,11... | collective-permute-start | bytes 294920 | tf_op jit(solution)/shard_map/ppermute | solution.py:338
  157.8 1.8 %collective-permute-start.59 = (f32[2,32,256]{2,1,0:T(8,128)S(1)}, f32[2,32,256]{2,1,0:T(8,128)S(1)}, u32[]{:S(2)}, u32[]{:S(2)}) collective-permute-start(f32[2,32,256]{2,1,0:T(8,128)S(1)} %get-tuple-element.107.rest_2_), channel_id=1, source_target_pairs={{0,3},{1,2},{2,1},{3,0},{4,7},{5,6},{6,5},{7,4},{8,11},{9,10},{10,... | collective-permute-start | bytes 196616 | tf_op jit(solution)/shard_map/ppermute | solution.py:338
  167.6 2.0 %collective-permute-start.67 = (f32[2,32,256]{2,1,0:T(8,128)S(1)}, f32[2,32,256]{2,1,0:T(8,128)S(1)}, u32[]{:S(2)}, u32[]{:S(2)}) collective-permute-start(f32[2,32,256]{2,1,0:T(8,128)S(1)} %get-tuple-element.117), channel_id=1, source_target_pairs={{0,24},{4,28},{8,16},{12,20},{16,8},{20,12},{24,0},{28,4},{1,25},{... | collective-permute-start | bytes 196616 | tf_op jit(solution)/shard_map/ppermute | solution.py:290
  171.1 1.7 collective-permute-done.67.rest_3_
  (147 shorter events, 86.3 us)
Async XLA Ops:
  3.6 5.3 %collective-permute-start.2 = (f32[2,32,256]{2,1,0:T(8,128)S(1)}, f32[2,32,256]{2,1,0:T(8,128)S(1)}, u32[]{:S(2)}, u32[]{:S(2)}) collective-permute-start(f32[2,32,256]{2,1,0:T(8,128)S(1)} %get-tuple-element.69.rest_9_), channel_id=1, source_target_pairs={{0,8},{4,12},{8,0},{12,4},{16,24},{20,28},{24,16},{28,20},{1,9},{5... | collective-permute-start | bytes 196616 | tf_op jit(solution)/shard_map/ppermute | solution.py:290
  8.0 5.2 %collective-permute-start.4 = (f32[2,32,256]{2,1,0:T(8,128)S(1)}, f32[2,32,256]{2,1,0:T(8,128)S(1)}, u32[]{:S(2)}, u32[]{:S(2)}) collective-permute-start(f32[2,32,256]{2,1,0:T(8,128)S(1)} %get-tuple-element.71.rest_11_), channel_id=1, source_target_pairs={{0,24},{4,28},{8,16},{12,20},{16,8},{20,12},{24,0},{28,4},{1,25},{... | collective-permute-start | bytes 196616 | tf_op jit(solution)/shard_map/ppermute | solution.py:290
  13.2 29.5 %collective-permute-start.10 = (f32[6,32,256]{2,1,0:T(8,128)S(1)}, f32[6,32,256]{2,1,0:T(8,128)S(1)}, u32[]{:S(2)}, u32[]{:S(2)}) collective-permute-start(f32[6,32,256]{2,1,0:T(8,128)S(1)} %shard_map.61.rest_1_), channel_id=1, source_target_pairs={{0,1},{1,0},{2,3},{3,2},{4,5},{5,4},{6,7},{7,6},{8,9},{9,8},{10,11... | collective-permute-start | bytes 589832 | tf_op jit(solution)/shard_map/ppermute | solution.py:338
  14.9 29.4 %collective-permute-start.8 = (f32[6,32,256]{2,1,0:T(8,128)S(1)}, f32[6,32,256]{2,1,0:T(8,128)S(1)}, u32[]{:S(2)}, u32[]{:S(2)}) collective-permute-start(f32[6,32,256]{2,1,0:T(8,128)S(1)} %shard_map.61.rest_1_), channel_id=1, source_target_pairs={{0,2},{1,3},{2,0},{3,1},{4,6},{5,7},{6,4},{7,5},{8,10},{9,11},{10,... | collective-permute-start | bytes 589832 | tf_op jit(solution)/shard_map/ppermute | solution.py:338
  17.4 28.4 %collective-permute-start.6 = (f32[6,32,256]{2,1,0:T(8,128)S(1)}, f32[6,32,256]{2,1,0:T(8,128)S(1)}, u32[]{:S(2)}, u32[]{:S(2)}) collective-permute-start(f32[6,32,256]{2,1,0:T(8,128)S(1)} %shard_map.61.rest_1_), channel_id=1, source_target_pairs={{0,3},{1,2},{2,1},{3,0},{4,7},{5,6},{6,5},{7,4},{8,11},{9,10},{10,... | collective-permute-start | bytes 589832 | tf_op jit(solution)/shard_map/ppermute | solution.py:338
  17.7 11.4 %collective-permute-start.9 = (f32[2,32,256]{2,1,0:T(8,128)S(1)}, f32[2,32,256]{2,1,0:T(8,128)S(1)}, u32[]{:S(2)}, u32[]{:S(2)}) collective-permute-start(f32[2,32,256]{2,1,0:T(8,128)S(1)} %get-tuple-element.68.rest_0_.rest_8_), channel_id=1, source_target_pairs={{0,1},{1,0},{2,3},{3,2},{4,5},{5,4},{6,7},{7,6},{8,9},{9,8},{10,11... | collective-permute-start | bytes 196616 | tf_op jit(solution)/shard_map/ppermute | solution.py:338
  18.3 25.9 %collective-permute-start.7 = (f32[2,32,256]{2,1,0:T(8,128)S(1)}, f32[2,32,256]{2,1,0:T(8,128)S(1)}, u32[]{:S(2)}, u32[]{:S(2)}) collective-permute-start(f32[2,32,256]{2,1,0:T(8,128)S(1)} %get-tuple-element.68.rest_0_.rest_8_), channel_id=1, source_target_pairs={{0,2},{1,3},{2,0},{3,1},{4,6},{5,7},{6,4},{7,5},{8,10},{9,11},{10,... | collective-permute-start | bytes 196616 | tf_op jit(solution)/shard_map/ppermute | solution.py:338
  29.1 16.8 %collective-permute-start.5 = (f32[2,32,256]{2,1,0:T(8,128)S(1)}, f32[2,32,256]{2,1,0:T(8,128)S(1)}, u32[]{:S(2)}, u32[]{:S(2)}) collective-permute-start(f32[2,32,256]{2,1,0:T(8,128)S(1)} %get-tuple-element.68.rest_0_.rest_8_), channel_id=1, source_target_pairs={{0,3},{1,2},{2,1},{3,0},{4,7},{5,6},{6,5},{7,4},{8,11},{9,10},{10,... | collective-permute-start | bytes 196616 | tf_op jit(solution)/shard_map/ppermute | solution.py:338
  64.4 17.7 %collective-permute-start.28 = (f32[6,32,256]{2,1,0:T(8,128)S(1)}, f32[6,32,256]{2,1,0:T(8,128)S(1)}, u32[]{:S(2)}, u32[]{:S(2)}) collective-permute-start(f32[6,32,256]{2,1,0:T(8,128)S(1)} %get-tuple-element.89.rest_3_), channel_id=1, source_target_pairs={{0,1},{1,0},{2,3},{3,2},{4,5},{5,4},{6,7},{7,6},{8,9},{9,8},{10,11... | collective-permute-start | bytes 589832 | tf_op jit(solution)/shard_map/ppermute | solution.py:338
  66.0 7.4 %collective-permute-start.24 = (f32[6,16,256]{2,1,0:T(8,128)S(1)}, f32[6,16,256]{2,1,0:T(8,128)S(1)}, u32[]{:S(2)}, u32[]{:S(2)}) collective-permute-start(f32[6,16,256]{2,1,0:T(8,128)S(1)} %get-tuple-element.88), channel_id=1, source_target_pairs={{0,2},{1,3},{2,0},{3,1},{4,6},{5,7},{6,4},{7,5},{8,10},{9,11},{10,... | collective-permute-start | bytes 294920 | tf_op jit(solution)/shard_map/ppermute | solution.py:338
  66.6 10.9 %collective-permute-start.18 = (f32[2,32,256]{2,1,0:T(8,128)S(1)}, f32[2,32,256]{2,1,0:T(8,128)S(1)}, u32[]{:S(2)}, u32[]{:S(2)}) collective-permute-start(f32[2,32,256]{2,1,0:T(8,128)S(1)} %get-tuple-element.83.rest_2_), channel_id=1, source_target_pairs={{0,2},{1,3},{2,0},{3,1},{4,6},{5,7},{6,4},{7,5},{8,10},{9,11},{10,... | collective-permute-start | bytes 196616 | tf_op jit(solution)/shard_map/ppermute | solution.py:338
  69.0 9.3 %collective-permute-start.27 = (f32[2,32,256]{2,1,0:T(8,128)S(1)}, f32[2,32,256]{2,1,0:T(8,128)S(1)}, u32[]{:S(2)}, u32[]{:S(2)}) collective-permute-start(f32[2,32,256]{2,1,0:T(8,128)S(1)} %get-tuple-element.83.rest_2_), channel_id=1, source_target_pairs={{0,1},{1,0},{2,3},{3,2},{4,5},{5,4},{6,7},{7,6},{8,9},{9,8},{10,11... | collective-permute-start | bytes 196616 | tf_op jit(solution)/shard_map/ppermute | solution.py:338
  69.4 15.0 %collective-permute-start.26 = (f32[6,16,256]{2,1,0:T(8,128)S(1)}, f32[6,16,256]{2,1,0:T(8,128)S(1)}, u32[]{:S(2)}, u32[]{:S(2)}) collective-permute-start(f32[6,16,256]{2,1,0:T(8,128)S(1)} %get-tuple-element.87), channel_id=1, source_target_pairs={{0,3},{1,2},{2,1},{3,0},{4,7},{5,6},{6,5},{7,4},{8,11},{9,10},{10,... | collective-permute-start | bytes 294920 | tf_op jit(solution)/shard_map/ppermute | solution.py:338
  73.5 11.7 %collective-permute-start.25 = (f32[6,16,256]{2,1,0:T(8,128)S(1)}, f32[6,16,256]{2,1,0:T(8,128)S(1)}, u32[]{:S(2)}, u32[]{:S(2)}) collective-permute-start(f32[6,16,256]{2,1,0:T(8,128)S(1)} %collective-permute-done.24.rest_3_), channel_id=1, source_target_pairs={{0,1},{1,0},{2,3},{3,2},{4,5},{5,4},{6,7},{7,6},{8,9},{9,8},{10,11... | collective-permute-start | bytes 294920 | tf_op jit(solution)/shard_map/ppermute | solution.py:338
  77.5 8.4 %collective-permute-start.22 = (f32[6,16,256]{2,1,0:T(8,128)S(1)}, f32[6,16,256]{2,1,0:T(8,128)S(1)}, u32[]{:S(2)}, u32[]{:S(2)}) collective-permute-start(f32[6,16,256]{2,1,0:T(8,128)S(1)} %get-tuple-element.87), channel_id=1, source_target_pairs={{0,2},{1,3},{2,0},{3,1},{4,6},{5,7},{6,4},{7,5},{8,10},{9,11},{10,... | collective-permute-start | bytes 294920 | tf_op jit(solution)/shard_map/ppermute | solution.py:338
  78.3 6.2 %collective-permute-start.23 = (f32[2,32,256]{2,1,0:T(8,128)S(1)}, f32[2,32,256]{2,1,0:T(8,128)S(1)}, u32[]{:S(2)}, u32[]{:S(2)}) collective-permute-start(f32[2,32,256]{2,1,0:T(8,128)S(1)} %get-tuple-element.83.rest_2_), channel_id=1, source_target_pairs={{0,3},{1,2},{2,1},{3,0},{4,7},{5,6},{6,5},{7,4},{8,11},{9,10},{10,... | collective-permute-start | bytes 196616 | tf_op jit(solution)/shard_map/ppermute | solution.py:338
  103.7 18.4 %collective-permute-start.46 = (f32[6,32,256]{2,1,0:T(8,128)S(1)}, f32[6,32,256]{2,1,0:T(8,128)S(1)}, u32[]{:S(2)}, u32[]{:S(2)}) collective-permute-start(f32[6,32,256]{2,1,0:T(8,128)S(1)} %get-tuple-element.102.rest_3_), channel_id=1, source_target_pairs={{0,1},{1,0},{2,3},{3,2},{4,5},{5,4},{6,7},{7,6},{8,9},{9,8},{10,11... | collective-permute-start | bytes 589832 | tf_op jit(solution)/shard_map/ppermute | solution.py:338
  105.8 7.4 %collective-permute-start.42 = (f32[6,16,256]{2,1,0:T(8,128)S(1)}, f32[6,16,256]{2,1,0:T(8,128)S(1)}, u32[]{:S(2)}, u32[]{:S(2)}) collective-permute-start(f32[6,16,256]{2,1,0:T(8,128)S(1)} %get-tuple-element.101), channel_id=1, source_target_pairs={{0,2},{1,3},{2,0},{3,1},{4,6},{5,7},{6,4},{7,5},{8,10},{9,11},{10,... | collective-permute-start | bytes 294920 | tf_op jit(solution)/shard_map/ppermute | solution.py:338
  106.2 10.9 %collective-permute-start.36 = (f32[2,32,256]{2,1,0:T(8,128)S(1)}, f32[2,32,256]{2,1,0:T(8,128)S(1)}, u32[]{:S(2)}, u32[]{:S(2)}) collective-permute-start(f32[2,32,256]{2,1,0:T(8,128)S(1)} %get-tuple-element.96.rest_2_), channel_id=1, source_target_pairs={{0,2},{1,3},{2,0},{3,1},{4,6},{5,7},{6,4},{7,5},{8,10},{9,11},{10,... | collective-permute-start | bytes 196616 | tf_op jit(solution)/shard_map/ppermute | solution.py:338
  108.7 9.3 %collective-permute-start.45 = (f32[2,32,256]{2,1,0:T(8,128)S(1)}, f32[2,32,256]{2,1,0:T(8,128)S(1)}, u32[]{:S(2)}, u32[]{:S(2)}) collective-permute-start(f32[2,32,256]{2,1,0:T(8,128)S(1)} %get-tuple-element.96.rest_2_), channel_id=1, source_target_pairs={{0,1},{1,0},{2,3},{3,2},{4,5},{5,4},{6,7},{7,6},{8,9},{9,8},{10,11... | collective-permute-start | bytes 196616 | tf_op jit(solution)/shard_map/ppermute | solution.py:338
  108.8 15.4 %collective-permute-start.44 = (f32[6,16,256]{2,1,0:T(8,128)S(1)}, f32[6,16,256]{2,1,0:T(8,128)S(1)}, u32[]{:S(2)}, u32[]{:S(2)}) collective-permute-start(f32[6,16,256]{2,1,0:T(8,128)S(1)} %get-tuple-element.100), channel_id=1, source_target_pairs={{0,3},{1,2},{2,1},{3,0},{4,7},{5,6},{6,5},{7,4},{8,11},{9,10},{10,... | collective-permute-start | bytes 294920 | tf_op jit(solution)/shard_map/ppermute | solution.py:338
  113.2 11.7 %collective-permute-start.43 = (f32[6,16,256]{2,1,0:T(8,128)S(1)}, f32[6,16,256]{2,1,0:T(8,128)S(1)}, u32[]{:S(2)}, u32[]{:S(2)}) collective-permute-start(f32[6,16,256]{2,1,0:T(8,128)S(1)} %collective-permute-done.42.rest_3_), channel_id=1, source_target_pairs={{0,1},{1,0},{2,3},{3,2},{4,5},{5,4},{6,7},{7,6},{8,9},{9,8},{10,11... | collective-permute-start | bytes 294920 | tf_op jit(solution)/shard_map/ppermute | solution.py:338
  117.1 8.5 %collective-permute-start.40 = (f32[6,16,256]{2,1,0:T(8,128)S(1)}, f32[6,16,256]{2,1,0:T(8,128)S(1)}, u32[]{:S(2)}, u32[]{:S(2)}) collective-permute-start(f32[6,16,256]{2,1,0:T(8,128)S(1)} %get-tuple-element.100), channel_id=1, source_target_pairs={{0,2},{1,3},{2,0},{3,1},{4,6},{5,7},{6,4},{7,5},{8,10},{9,11},{10,... | collective-permute-start | bytes 294920 | tf_op jit(solution)/shard_map/ppermute | solution.py:338
  118.0 6.2 %collective-permute-start.41 = (f32[2,32,256]{2,1,0:T(8,128)S(1)}, f32[2,32,256]{2,1,0:T(8,128)S(1)}, u32[]{:S(2)}, u32[]{:S(2)}) collective-permute-start(f32[2,32,256]{2,1,0:T(8,128)S(1)} %get-tuple-element.96.rest_2_), channel_id=1, source_target_pairs={{0,3},{1,2},{2,1},{3,0},{4,7},{5,6},{6,5},{7,4},{8,11},{9,10},{10,... | collective-permute-start | bytes 196616 | tf_op jit(solution)/shard_map/ppermute | solution.py:338
  143.4 18.5 %collective-permute-start.64 = (f32[6,32,256]{2,1,0:T(8,128)S(1)}, f32[6,32,256]{2,1,0:T(8,128)S(1)}, u32[]{:S(2)}, u32[]{:S(2)}) collective-permute-start(f32[6,32,256]{2,1,0:T(8,128)S(1)} %get-tuple-element.113.rest_3_), channel_id=1, source_target_pairs={{0,1},{1,0},{2,3},{3,2},{4,5},{5,4},{6,7},{7,6},{8,9},{9,8},{10,11... | collective-permute-start | bytes 589832 | tf_op jit(solution)/shard_map/ppermute | solution.py:338
  145.6 7.4 %collective-permute-start.60 = (f32[6,16,256]{2,1,0:T(8,128)S(1)}, f32[6,16,256]{2,1,0:T(8,128)S(1)}, u32[]{:S(2)}, u32[]{:S(2)}) collective-permute-start(f32[6,16,256]{2,1,0:T(8,128)S(1)} %get-tuple-element.112), channel_id=1, source_target_pairs={{0,2},{1,3},{2,0},{3,1},{4,6},{5,7},{6,4},{7,5},{8,10},{9,11},{10,... | collective-permute-start | bytes 294920 | tf_op jit(solution)/shard_map/ppermute | solution.py:338
  146.0 10.8 %collective-permute-start.54 = (f32[2,32,256]{2,1,0:T(8,128)S(1)}, f32[2,32,256]{2,1,0:T(8,128)S(1)}, u32[]{:S(2)}, u32[]{:S(2)}) collective-permute-start(f32[2,32,256]{2,1,0:T(8,128)S(1)} %get-tuple-element.107.rest_2_), channel_id=1, source_target_pairs={{0,2},{1,3},{2,0},{3,1},{4,6},{5,7},{6,4},{7,5},{8,10},{9,11},{10,... | collective-permute-start | bytes 196616 | tf_op jit(solution)/shard_map/ppermute | solution.py:338
  148.5 9.3 %collective-permute-start.63 = (f32[2,32,256]{2,1,0:T(8,128)S(1)}, f32[2,32,256]{2,1,0:T(8,128)S(1)}, u32[]{:S(2)}, u32[]{:S(2)}) collective-permute-start(f32[2,32,256]{2,1,0:T(8,128)S(1)} %get-tuple-element.107.rest_2_), channel_id=1, source_target_pairs={{0,1},{1,0},{2,3},{3,2},{4,5},{5,4},{6,7},{7,6},{8,9},{9,8},{10,11... | collective-permute-start | bytes 196616 | tf_op jit(solution)/shard_map/ppermute | solution.py:338
  148.6 15.3 %collective-permute-start.62 = (f32[6,16,256]{2,1,0:T(8,128)S(1)}, f32[6,16,256]{2,1,0:T(8,128)S(1)}, u32[]{:S(2)}, u32[]{:S(2)}) collective-permute-start(f32[6,16,256]{2,1,0:T(8,128)S(1)} %get-tuple-element.111), channel_id=1, source_target_pairs={{0,3},{1,2},{2,1},{3,0},{4,7},{5,6},{6,5},{7,4},{8,11},{9,10},{10,... | collective-permute-start | bytes 294920 | tf_op jit(solution)/shard_map/ppermute | solution.py:338
  153.0 11.6 %collective-permute-start.61 = (f32[6,16,256]{2,1,0:T(8,128)S(1)}, f32[6,16,256]{2,1,0:T(8,128)S(1)}, u32[]{:S(2)}, u32[]{:S(2)}) collective-permute-start(f32[6,16,256]{2,1,0:T(8,128)S(1)} %collective-permute-done.60.rest_3_), channel_id=1, source_target_pairs={{0,1},{1,0},{2,3},{3,2},{4,5},{5,4},{6,7},{7,6},{8,9},{9,8},{10,11... | collective-permute-start | bytes 294920 | tf_op jit(solution)/shard_map/ppermute | solution.py:338
  156.8 8.6 %collective-permute-start.58 = (f32[6,16,256]{2,1,0:T(8,128)S(1)}, f32[6,16,256]{2,1,0:T(8,128)S(1)}, u32[]{:S(2)}, u32[]{:S(2)}) collective-permute-start(f32[6,16,256]{2,1,0:T(8,128)S(1)} %get-tuple-element.111), channel_id=1, source_target_pairs={{0,2},{1,3},{2,0},{3,1},{4,6},{5,7},{6,4},{7,5},{8,10},{9,11},{10,... | collective-permute-start | bytes 294920 | tf_op jit(solution)/shard_map/ppermute | solution.py:338
  157.8 6.1 %collective-permute-start.59 = (f32[2,32,256]{2,1,0:T(8,128)S(1)}, f32[2,32,256]{2,1,0:T(8,128)S(1)}, u32[]{:S(2)}, u32[]{:S(2)}) collective-permute-start(f32[2,32,256]{2,1,0:T(8,128)S(1)} %get-tuple-element.107.rest_2_), channel_id=1, source_target_pairs={{0,3},{1,2},{2,1},{3,0},{4,7},{5,6},{6,5},{7,4},{8,11},{9,10},{10,... | collective-permute-start | bytes 196616 | tf_op jit(solution)/shard_map/ppermute | solution.py:338
  (41 other events, 149.5 us)

commit v2 on v1

--- a/solution.py
+++ b/solution.py
@@ -264,7 +264,7 @@
         ]
         if not here and not chips:
             continue
-        step = math.gcd(end - begin, max(1, 8 // max(1, len(here))))
+        step = math.gcd(end - begin, max(1, 16 // max(1, len(here))))
 
         @pl.loop(begin // step, end // step)
         def _(i):
@@ -348,7 +348,7 @@
             c1 = shift(high, 3)
             b1 = shift(high, 2)
             c0 = shift(b0, 1)
-            pieces = [(0, 0, x), (2, 0, b0), (1, 0, a), (3, half, c1), (3, 0, c0), (2, half, b1)]
+            pieces = [(0, 0, x), (2, 0, b0), (3, half, c1), (1, 0, a), (2, half, b1), (3, 0, c0)]
         return [
             [(b, at, [near[b], array] if near else [array])] for b, at, array in pieces
         ]
@@ -366,9 +366,9 @@
             out_specs=(VMEM,) * (2 * z_size + 1),
             out_shape=(pltpu.VMEM(shape, BF16),) * (2 * z_size)
             + (sds((n, 2, points, rows), F32),),
-            scratch_shapes=[pltpu.VMEM((4, 2, rows, receivers), F32), pltpu.SemaphoreType.DMA((4,))]
+            scratch_shapes=[pltpu.VMEM((6, 2, rows, receivers), F32), pltpu.SemaphoreType.DMA((6,))]
             + field_scratch(arrays),
-            compiler_params=pltpu.CompilerParams(vmem_limit_bytes=12 << 20),
+            compiler_params=pltpu.CompilerParams(vmem_limit_bytes=16 << 20),
         )(kernel, place, *arrays)
         return outs, [total]
 

time: 176 us -> 185 us (1.051)
  waiting for transfers between devices: 54.7 us -> 71 us
  starting transfers between devices: 77.5 us -> 72.5 us
    ppermute x30, waiting for transfers between devices: 20.2 us -> 36.5 us  [shift(): return lax.ppermute(x, 'rcv', [(i, i ^ d) for i in range(z_size)])]
    ppermute x30, starting transfers between devices: 47.5 us -> 42.5 us  [shift(): return lax.ppermute(x, 'rcv', [(i, i ^ d) for i in range(z_size)])]
  transfers between devices with their start and end apart: 72 -> 72, of which waited for: 38 -> 35; matrix products, arithmetic and copies ran while one was open for 0% -> 0% of each run, Pallas kernels for 19% -> 17%
where the time goes in v2:
time: 185 us
  starting transfers between devices  72.5 us (39%)
  waiting for transfers between devices  71 us (38%)
  Pallas kernels  40.7 us (22%)
    ppermute x30, starting transfers between devices, shift(): return lax.ppermute(x, 'rcv', [(i, i ^ d) for i in range(z_size)])  42.5 us
    ppermute x30, waiting for transfers between devices, shift(): return lax.ppermute(x, 'rcv', [(i, i ^ d) for i in range(z_size)])  36.5 us
    ppermute x42, waiting for transfers between devices, trade(): return lax.ppermute(x, 'freq', [(i, i ^ d) for i in range(n_f)])  34.5 us
    ppermute x42, starting transfers between devices, trade(): return lax.ppermute(x, 'freq', [(i, i ^ d) for i in range(n_f)])  30 us
    pallas_call x32, Pallas kernels, call(): pl.pallas_call(body, in_specs=ins, out_specs=tuple((VMEM for _ in outs)),...  29.1 us
    pallas_call x1, Pallas kernels, hold(): pl.pallas_call(functools.partial(hold_body, z_size, parity, len(arrays)),...  11.6 us
  transfers between devices with their start and end apart: 72, of which 35 were waited for; matrix products, arithmetic and copies ran while one was open for 0% of the time, Pallas kernels for 17%

profile of v2, /device:TPU:0, one launch (start us, length us, event | category | flops | bytes accessed | tf_op | source)
XLA Modules:
  0.0 185.2 jit_solution(14655896406623259258)
XLA Ops:
  3.6 2.9 %collective-permute-start.2 = (f32[2,32,256]{2,1,0:T(8,128)S(1)}, f32[2,32,256]{2,1,0:T(8,128)S(1)}, u32[]{:S(2)}, u32[]{:S(2)}) collective-permute-start(f32[2,32,256]{2,1,0:T(8,128)S(1)} %get-tuple-element.69.rest_9_), channel_id=1, source_target_pairs={{0,8},{4,12},{8,0},{12,4},{16,24},{20,28},{24,16},{28,20},{1,9},{5... | collective-permute-start | bytes 196616 | tf_op jit(solution)/shard_map/ppermute | solution.py:290
  8.9 1.9 %collective-permute-done.3.rest_1_ = f32[2,32,256]{2,1,0:T(8,128)S(1)} collective-permute-done((f32[2,32,256]{2,1,0:T(8,128)S(1)}, f32[2,32,256]{2,1,0:T(8,128)S(1)}, u32[]{:S(2)}, u32[]{:S(2)}) %collective-permute-start.3) | collective-permute-done | bytes 65568 | tf_op jit(solution)/shard_map/ppermute | solution.py:290
  10.8 2.4 %collective-permute-done.4.rest_2_ = f32[2,32,256]{2,1,0:T(8,128)S(1)} collective-permute-done((f32[2,32,256]{2,1,0:T(8,128)S(1)}, f32[2,32,256]{2,1,0:T(8,128)S(1)}, u32[]{:S(2)}, u32[]{:S(2)}) %collective-permute-start.4) | collective-permute-done | bytes 65568 | tf_op jit(solution)/shard_map/ppermute | solution.py:290
  13.2 1.6 collective-permute-start.10
  14.9 2.6 %collective-permute-start.8 = (f32[6,32,256]{2,1,0:T(8,128)S(1)}, f32[6,32,256]{2,1,0:T(8,128)S(1)}, u32[]{:S(2)}, u32[]{:S(2)}) collective-permute-start(f32[6,32,256]{2,1,0:T(8,128)S(1)} %shard_map.61.rest_1_), channel_id=1, source_target_pairs={{0,2},{1,3},{2,0},{3,1},{4,6},{5,7},{6,4},{7,5},{8,10},{9,11},{10,... | collective-permute-start | bytes 589832 | tf_op jit(solution)/shard_map/ppermute | solution.py:338
  18.3 3.5 %collective-permute-start.7 = (f32[2,32,256]{2,1,0:T(8,128)S(1)}, f32[2,32,256]{2,1,0:T(8,128)S(1)}, u32[]{:S(2)}, u32[]{:S(2)}) collective-permute-start(f32[2,32,256]{2,1,0:T(8,128)S(1)} %get-tuple-element.68.rest_0_.rest_8_), channel_id=1, source_target_pairs={{0,2},{1,3},{2,0},{3,1},{4,6},{5,7},{6,4},{7,5},{8,10},{9,11},{10,... | collective-permute-start | bytes 196616 | tf_op jit(solution)/shard_map/ppermute | solution.py:338
  21.8 7.2 %collective-permute-done.9.rest_2_ = f32[2,32,256]{2,1,0:T(8,128)S(1)} collective-permute-done((f32[2,32,256]{2,1,0:T(8,128)S(1)}, f32[2,32,256]{2,1,0:T(8,128)S(1)}, u32[]{:S(2)}, u32[]{:S(2)}) %collective-permute-start.9) | collective-permute-done | bytes 65568 | tf_op jit(solution)/shard_map/ppermute | solution.py:338
  29.1 2.3 %collective-permute-start.5 = (f32[2,32,256]{2,1,0:T(8,128)S(1)}, f32[2,32,256]{2,1,0:T(8,128)S(1)}, u32[]{:S(2)}, u32[]{:S(2)}) collective-permute-start(f32[2,32,256]{2,1,0:T(8,128)S(1)} %get-tuple-element.68.rest_0_.rest_8_), channel_id=1, source_target_pairs={{0,3},{1,2},{2,1},{3,0},{4,7},{5,6},{6,5},{7,4},{8,11},{9,10},{10,... | collective-permute-start | bytes 196616 | tf_op jit(solution)/shard_map/ppermute | solution.py:338
  31.3 11.6 %shard_map.62 = (bf16[2,16,256,256]{3,2,1,0:T(8,128)(2,1)S(1)}, bf16[2,16,256,256]{3,2,1,0:T(8,128)(2,1)S(1)}, bf16[2,16,256,256]{3,2,1,0:T(8,128)(2,1)S(1)}, bf...) custom-call(f32[2,16,256,1024]{3,2,1,0:T(8,128)} %kernel.1, ...), custom_call_target="tpu_custom_call" | custom-call | tf_op jit(solution)/shard_map/pallas_call | solution.py:363
  48.3 2.3 %collective-permute-start.13 = (f32[2,32,256]{2,1,0:T(8,128)S(1)}, f32[2,32,256]{2,1,0:T(8,128)S(1)}, u32[]{:S(2)}, u32[]{:S(2)}) collective-permute-start(f32[2,32,256]{2,1,0:T(8,128)S(1)} %get-tuple-element.82), channel_id=1, source_target_pairs={{0,24},{4,28},{8,16},{12,20},{16,8},{20,12},{24,0},{28,4},{1,25},{... | collective-permute-start | bytes 196616 | tf_op jit(solution)/shard_map/ppermute | solution.py:290
  61.6 2.3 %collective-permute-done.21.rest_2_ = f32[2,32,256]{2,1,0:T(8,128)S(1)} collective-permute-done((f32[2,32,256]{2,1,0:T(8,128)S(1)}, f32[2,32,256]{2,1,0:T(8,128)S(1)}, u32[]{:S(2)}, u32[]{:S(2)}) %collective-permute-start.21) | collective-permute-done | bytes 65568 | tf_op jit(solution)/shard_map/ppermute | solution.py:290
  63.9 1.7 collective-permute-start.27
  66.1 2.4 %collective-permute-start.24 = (f32[2,32,256]{2,1,0:T(8,128)S(1)}, f32[2,32,256]{2,1,0:T(8,128)S(1)}, u32[]{:S(2)}, u32[]{:S(2)}) collective-permute-start(f32[2,32,256]{2,1,0:T(8,128)S(1)} %get-tuple-element.83.rest_2_), channel_id=1, source_target_pairs={{0,2},{1,3},{2,0},{3,1},{4,6},{5,7},{6,4},{7,5},{8,10},{9,11},{10,... | collective-permute-start | bytes 196616 | tf_op jit(solution)/shard_map/ppermute | solution.py:338
  70.1 2.3 %collective-permute-start.28 = (f32[6,16,256]{2,1,0:T(8,128)S(1)}, f32[6,16,256]{2,1,0:T(8,128)S(1)}, u32[]{:S(2)}, u32[]{:S(2)}) collective-permute-start(f32[6,16,256]{2,1,0:T(8,128)S(1)} %get-tuple-element.88), channel_id=1, source_target_pairs={{0,3},{1,2},{2,1},{3,0},{4,7},{5,6},{6,5},{7,4},{8,11},{9,10},{10,... | collective-permute-start | bytes 294920 | tf_op jit(solution)/shard_map/ppermute | solution.py:338
  72.3 8.2 %collective-permute-done.24.rest_2_ = f32[2,32,256]{2,1,0:T(8,128)S(1)} collective-permute-done((f32[2,32,256]{2,1,0:T(8,128)S(1)}, f32[2,32,256]{2,1,0:T(8,128)S(1)}, u32[]{:S(2)}, u32[]{:S(2)}) %collective-permute-start.24) | collective-permute-done | bytes 65568 | tf_op jit(solution)/shard_map/ppermute | solution.py:338
  80.5 2.5 %collective-permute-start.23 = (f32[6,16,256]{2,1,0:T(8,128)S(1)}, f32[6,16,256]{2,1,0:T(8,128)S(1)}, u32[]{:S(2)}, u32[]{:S(2)}) collective-permute-start(f32[6,16,256]{2,1,0:T(8,128)S(1)} %collective-permute-done.22.rest_3_), channel_id=1, source_target_pairs={{0,1},{1,0},{2,3},{3,2},{4,5},{5,4},{6,7},{7,6},{8,9},{9,8},{10,11... | collective-permute-start | bytes 294920 | tf_op jit(solution)/shard_map/ppermute | solution.py:338
  91.5 2.2 %collective-permute-start.31 = (f32[2,32,256]{2,1,0:T(8,128)S(1)}, f32[2,32,256]{2,1,0:T(8,128)S(1)}, u32[]{:S(2)}, u32[]{:S(2)}) collective-permute-start(f32[2,32,256]{2,1,0:T(8,128)S(1)} %get-tuple-element.95), channel_id=1, source_target_pairs={{0,24},{4,28},{8,16},{12,20},{16,8},{20,12},{24,0},{28,4},{1,25},{... | collective-permute-start | bytes 196616 | tf_op jit(solution)/shard_map/ppermute | solution.py:290
  95.1 1.6 collective-permute-done.31.rest_3_
  104.9 2.3 %collective-permute-done.39.rest_2_ = f32[2,32,256]{2,1,0:T(8,128)S(1)} collective-permute-done((f32[2,32,256]{2,1,0:T(8,128)S(1)}, f32[2,32,256]{2,1,0:T(8,128)S(1)}, u32[]{:S(2)}, u32[]{:S(2)}) %collective-permute-start.39) | collective-permute-done | bytes 65568 | tf_op jit(solution)/shard_map/ppermute | solution.py:290
  111.1 1.9 %collective-permute-start.36 = (f32[2,32,256]{2,1,0:T(8,128)S(1)}, f32[2,32,256]{2,1,0:T(8,128)S(1)}, u32[]{:S(2)}, u32[]{:S(2)}) collective-permute-start(f32[2,32,256]{2,1,0:T(8,128)S(1)} %get-tuple-element.96.rest_2_), channel_id=1, source_target_pairs={{0,3},{1,2},{2,1},{3,0},{4,7},{5,6},{6,5},{7,4},{8,11},{9,10},{10,... | collective-permute-start | bytes 196616 | tf_op jit(solution)/shard_map/ppermute | solution.py:338
  113.0 1.9 %collective-permute-start.46 = (f32[6,16,256]{2,1,0:T(8,128)S(1)}, f32[6,16,256]{2,1,0:T(8,128)S(1)}, u32[]{:S(2)}, u32[]{:S(2)}) collective-permute-start(f32[6,16,256]{2,1,0:T(8,128)S(1)} %get-tuple-element.101), channel_id=1, source_target_pairs={{0,3},{1,2},{2,1},{3,0},{4,7},{5,6},{6,5},{7,4},{8,11},{9,10},{10,... | collective-permute-start | bytes 294920 | tf_op jit(solution)/shard_map/ppermute | solution.py:338
  115.0 8.4 %collective-permute-done.42.rest_2_ = f32[2,32,256]{2,1,0:T(8,128)S(1)} collective-permute-done((f32[2,32,256]{2,1,0:T(8,128)S(1)}, f32[2,32,256]{2,1,0:T(8,128)S(1)}, u32[]{:S(2)}, u32[]{:S(2)}) %collective-permute-start.42) | collective-permute-done | bytes 65568 | tf_op jit(solution)/shard_map/ppermute | solution.py:338
  123.3 2.5 %collective-permute-start.41 = (f32[6,16,256]{2,1,0:T(8,128)S(1)}, f32[6,16,256]{2,1,0:T(8,128)S(1)}, u32[]{:S(2)}, u32[]{:S(2)}) collective-permute-start(f32[6,16,256]{2,1,0:T(8,128)S(1)} %collective-permute-done.40.rest_3_), channel_id=1, source_target_pairs={{0,1},{1,0},{2,3},{3,2},{4,5},{5,4},{6,7},{7,6},{8,9},{9,8},{10,11... | collective-permute-start | bytes 294920 | tf_op jit(solution)/shard_map/ppermute | solution.py:338
  134.4 2.1 %collective-permute-start.49 = (f32[2,32,256]{2,1,0:T(8,128)S(1)}, f32[2,32,256]{2,1,0:T(8,128)S(1)}, u32[]{:S(2)}, u32[]{:S(2)}) collective-permute-start(f32[2,32,256]{2,1,0:T(8,128)S(1)} %get-tuple-element.106), channel_id=1, source_target_pairs={{0,24},{4,28},{8,16},{12,20},{16,8},{20,12},{24,0},{28,4},{1,25},{... | collective-permute-start | bytes 196616 | tf_op jit(solution)/shard_map/ppermute | solution.py:290
  137.9 1.7 collective-permute-done.49.rest_3_
  147.8 2.2 %collective-permute-done.57.rest_2_ = f32[2,32,256]{2,1,0:T(8,128)S(1)} collective-permute-done((f32[2,32,256]{2,1,0:T(8,128)S(1)}, f32[2,32,256]{2,1,0:T(8,128)S(1)}, u32[]{:S(2)}, u32[]{:S(2)}) %collective-permute-start.57) | collective-permute-done | bytes 65568 | tf_op jit(solution)/shard_map/ppermute | solution.py:290
  153.9 1.9 %collective-permute-start.54 = (f32[2,32,256]{2,1,0:T(8,128)S(1)}, f32[2,32,256]{2,1,0:T(8,128)S(1)}, u32[]{:S(2)}, u32[]{:S(2)}) collective-permute-start(f32[2,32,256]{2,1,0:T(8,128)S(1)} %get-tuple-element.107.rest_2_), channel_id=1, source_target_pairs={{0,3},{1,2},{2,1},{3,0},{4,7},{5,6},{6,5},{7,4},{8,11},{9,10},{10,... | collective-permute-start | bytes 196616 | tf_op jit(solution)/shard_map/ppermute | solution.py:338
  155.8 1.9 %collective-permute-start.64 = (f32[6,16,256]{2,1,0:T(8,128)S(1)}, f32[6,16,256]{2,1,0:T(8,128)S(1)}, u32[]{:S(2)}, u32[]{:S(2)}) collective-permute-start(f32[6,16,256]{2,1,0:T(8,128)S(1)} %get-tuple-element.112), channel_id=1, source_target_pairs={{0,3},{1,2},{2,1},{3,0},{4,7},{5,6},{6,5},{7,4},{8,11},{9,10},{10,... | collective-permute-start | bytes 294920 | tf_op jit(solution)/shard_map/ppermute | solution.py:338
  157.8 8.4 %collective-permute-done.60.rest_2_ = f32[2,32,256]{2,1,0:T(8,128)S(1)} collective-permute-done((f32[2,32,256]{2,1,0:T(8,128)S(1)}, f32[2,32,256]{2,1,0:T(8,128)S(1)}, u32[]{:S(2)}, u32[]{:S(2)}) %collective-permute-start.60) | collective-permute-done | bytes 65568 | tf_op jit(solution)/shard_map/ppermute | solution.py:338
  166.1 2.5 %collective-permute-start.59 = (f32[6,16,256]{2,1,0:T(8,128)S(1)}, f32[6,16,256]{2,1,0:T(8,128)S(1)}, u32[]{:S(2)}, u32[]{:S(2)}) collective-permute-start(f32[6,16,256]{2,1,0:T(8,128)S(1)} %collective-permute-done.58.rest_3_), channel_id=1, source_target_pairs={{0,1},{1,0},{2,3},{3,2},{4,5},{5,4},{6,7},{7,6},{8,9},{9,8},{10,11... | collective-permute-start | bytes 294920 | tf_op jit(solution)/shard_map/ppermute | solution.py:338
  177.3 2.0 %collective-permute-start.67 = (f32[2,32,256]{2,1,0:T(8,128)S(1)}, f32[2,32,256]{2,1,0:T(8,128)S(1)}, u32[]{:S(2)}, u32[]{:S(2)}) collective-permute-start(f32[2,32,256]{2,1,0:T(8,128)S(1)} %get-tuple-element.117), channel_id=1, source_target_pairs={{0,24},{4,28},{8,16},{12,20},{16,8},{20,12},{24,0},{28,4},{1,25},{... | collective-permute-start | bytes 196616 | tf_op jit(solution)/shard_map/ppermute | solution.py:290
  180.7 1.8 collective-permute-done.67.rest_3_
  (147 shorter events, 81.6 us)
Async XLA Ops:
  3.6 5.3 %collective-permute-start.2 = (f32[2,32,256]{2,1,0:T(8,128)S(1)}, f32[2,32,256]{2,1,0:T(8,128)S(1)}, u32[]{:S(2)}, u32[]{:S(2)}) collective-permute-start(f32[2,32,256]{2,1,0:T(8,128)S(1)} %get-tuple-element.69.rest_9_), channel_id=1, source_target_pairs={{0,8},{4,12},{8,0},{12,4},{16,24},{20,28},{24,16},{28,20},{1,9},{5... | collective-permute-start | bytes 196616 | tf_op jit(solution)/shard_map/ppermute | solution.py:290
  8.0 5.2 %collective-permute-start.4 = (f32[2,32,256]{2,1,0:T(8,128)S(1)}, f32[2,32,256]{2,1,0:T(8,128)S(1)}, u32[]{:S(2)}, u32[]{:S(2)}) collective-permute-start(f32[2,32,256]{2,1,0:T(8,128)S(1)} %get-tuple-element.71.rest_11_), channel_id=1, source_target_pairs={{0,24},{4,28},{8,16},{12,20},{16,8},{20,12},{24,0},{28,4},{1,25},{... | collective-permute-start | bytes 196616 | tf_op jit(solution)/shard_map/ppermute | solution.py:290
  13.2 29.7 %collective-permute-start.10 = (f32[6,32,256]{2,1,0:T(8,128)S(1)}, f32[6,32,256]{2,1,0:T(8,128)S(1)}, u32[]{:S(2)}, u32[]{:S(2)}) collective-permute-start(f32[6,32,256]{2,1,0:T(8,128)S(1)} %shard_map.61.rest_1_), channel_id=1, source_target_pairs={{0,1},{1,0},{2,3},{3,2},{4,5},{5,4},{6,7},{7,6},{8,9},{9,8},{10,11... | collective-permute-start | bytes 589832 | tf_op jit(solution)/shard_map/ppermute | solution.py:338
  14.9 29.4 %collective-permute-start.8 = (f32[6,32,256]{2,1,0:T(8,128)S(1)}, f32[6,32,256]{2,1,0:T(8,128)S(1)}, u32[]{:S(2)}, u32[]{:S(2)}) collective-permute-start(f32[6,32,256]{2,1,0:T(8,128)S(1)} %shard_map.61.rest_1_), channel_id=1, source_target_pairs={{0,2},{1,3},{2,0},{3,1},{4,6},{5,7},{6,4},{7,5},{8,10},{9,11},{10,... | collective-permute-start | bytes 589832 | tf_op jit(solution)/shard_map/ppermute | solution.py:338
  17.4 28.2 %collective-permute-start.6 = (f32[6,32,256]{2,1,0:T(8,128)S(1)}, f32[6,32,256]{2,1,0:T(8,128)S(1)}, u32[]{:S(2)}, u32[]{:S(2)}) collective-permute-start(f32[6,32,256]{2,1,0:T(8,128)S(1)} %shard_map.61.rest_1_), channel_id=1, source_target_pairs={{0,3},{1,2},{2,1},{3,0},{4,7},{5,6},{6,5},{7,4},{8,11},{9,10},{10,... | collective-permute-start | bytes 589832 | tf_op jit(solution)/shard_map/ppermute | solution.py:338
  17.7 11.4 %collective-permute-start.9 = (f32[2,32,256]{2,1,0:T(8,128)S(1)}, f32[2,32,256]{2,1,0:T(8,128)S(1)}, u32[]{:S(2)}, u32[]{:S(2)}) collective-permute-start(f32[2,32,256]{2,1,0:T(8,128)S(1)} %get-tuple-element.68.rest_0_.rest_8_), channel_id=1, source_target_pairs={{0,1},{1,0},{2,3},{3,2},{4,5},{5,4},{6,7},{7,6},{8,9},{9,8},{10,11... | collective-permute-start | bytes 196616 | tf_op jit(solution)/shard_map/ppermute | solution.py:338
  18.3 25.9 %collective-permute-start.7 = (f32[2,32,256]{2,1,0:T(8,128)S(1)}, f32[2,32,256]{2,1,0:T(8,128)S(1)}, u32[]{:S(2)}, u32[]{:S(2)}) collective-permute-start(f32[2,32,256]{2,1,0:T(8,128)S(1)} %get-tuple-element.68.rest_0_.rest_8_), channel_id=1, source_target_pairs={{0,2},{1,3},{2,0},{3,1},{4,6},{5,7},{6,4},{7,5},{8,10},{9,11},{10,... | collective-permute-start | bytes 196616 | tf_op jit(solution)/shard_map/ppermute | solution.py:338
  29.1 16.5 %collective-permute-start.5 = (f32[2,32,256]{2,1,0:T(8,128)S(1)}, f32[2,32,256]{2,1,0:T(8,128)S(1)}, u32[]{:S(2)}, u32[]{:S(2)}) collective-permute-start(f32[2,32,256]{2,1,0:T(8,128)S(1)} %get-tuple-element.68.rest_0_.rest_8_), channel_id=1, source_target_pairs={{0,3},{1,2},{2,1},{3,0},{4,7},{5,6},{6,5},{7,4},{8,11},{9,10},{10,... | collective-permute-start | bytes 196616 | tf_op jit(solution)/shard_map/ppermute | solution.py:338
  48.3 5.2 %collective-permute-start.13 = (f32[2,32,256]{2,1,0:T(8,128)S(1)}, f32[2,32,256]{2,1,0:T(8,128)S(1)}, u32[]{:S(2)}, u32[]{:S(2)}) collective-permute-start(f32[2,32,256]{2,1,0:T(8,128)S(1)} %get-tuple-element.82), channel_id=1, source_target_pairs={{0,24},{4,28},{8,16},{12,20},{16,8},{20,12},{24,0},{28,4},{1,25},{... | collective-permute-start | bytes 196616 | tf_op jit(solution)/shard_map/ppermute | solution.py:290
  58.8 5.2 %collective-permute-start.21 = (f32[2,32,256]{2,1,0:T(8,128)S(1)}, f32[2,32,256]{2,1,0:T(8,128)S(1)}, u32[]{:S(2)}, u32[]{:S(2)}) collective-permute-start(f32[2,32,256]{2,1,0:T(8,128)S(1)} %get-tuple-element.86), channel_id=1, source_target_pairs={{0,24},{4,28},{8,16},{12,20},{16,8},{20,12},{24,0},{28,4},{1,25},{... | collective-permute-start | bytes 196616 | tf_op jit(solution)/shard_map/ppermute | solution.py:290
  63.9 23.4 %collective-permute-start.27 = (f32[6,32,256]{2,1,0:T(8,128)S(1)}, f32[6,32,256]{2,1,0:T(8,128)S(1)}, u32[]{:S(2)}, u32[]{:S(2)}) collective-permute-start(f32[6,32,256]{2,1,0:T(8,128)S(1)} %get-tuple-element.89.rest_3_), channel_id=1, source_target_pairs={{0,1},{1,0},{2,3},{3,2},{4,5},{5,4},{6,7},{7,6},{8,9},{9,8},{10,11... | collective-permute-start | bytes 589832 | tf_op jit(solution)/shard_map/ppermute | solution.py:338
  65.6 14.9 %collective-permute-start.22 = (f32[6,16,256]{2,1,0:T(8,128)S(1)}, f32[6,16,256]{2,1,0:T(8,128)S(1)}, u32[]{:S(2)}, u32[]{:S(2)}) collective-permute-start(f32[6,16,256]{2,1,0:T(8,128)S(1)} %get-tuple-element.87), channel_id=1, source_target_pairs={{0,2},{1,3},{2,0},{3,1},{4,6},{5,7},{6,4},{7,5},{8,10},{9,11},{10,... | collective-permute-start | bytes 294920 | tf_op jit(solution)/shard_map/ppermute | solution.py:338
  66.1 14.4 %collective-permute-start.24 = (f32[2,32,256]{2,1,0:T(8,128)S(1)}, f32[2,32,256]{2,1,0:T(8,128)S(1)}, u32[]{:S(2)}, u32[]{:S(2)}) collective-permute-start(f32[2,32,256]{2,1,0:T(8,128)S(1)} %get-tuple-element.83.rest_2_), channel_id=1, source_target_pairs={{0,2},{1,3},{2,0},{3,1},{4,6},{5,7},{6,4},{7,5},{8,10},{9,11},{10,... | collective-permute-start | bytes 196616 | tf_op jit(solution)/shard_map/ppermute | solution.py:338
  68.5 14.5 %collective-permute-start.18 = (f32[2,32,256]{2,1,0:T(8,128)S(1)}, f32[2,32,256]{2,1,0:T(8,128)S(1)}, u32[]{:S(2)}, u32[]{:S(2)}) collective-permute-start(f32[2,32,256]{2,1,0:T(8,128)S(1)} %get-tuple-element.83.rest_2_), channel_id=1, source_target_pairs={{0,3},{1,2},{2,1},{3,0},{4,7},{5,6},{6,5},{7,4},{8,11},{9,10},{10,... | collective-permute-start | bytes 196616 | tf_op jit(solution)/shard_map/ppermute | solution.py:338
  70.1 15.1 %collective-permute-start.28 = (f32[6,16,256]{2,1,0:T(8,128)S(1)}, f32[6,16,256]{2,1,0:T(8,128)S(1)}, u32[]{:S(2)}, u32[]{:S(2)}) collective-permute-start(f32[6,16,256]{2,1,0:T(8,128)S(1)} %get-tuple-element.88), channel_id=1, source_target_pairs={{0,3},{1,2},{2,1},{3,0},{4,7},{5,6},{6,5},{7,4},{8,11},{9,10},{10,... | collective-permute-start | bytes 294920 | tf_op jit(solution)/shard_map/ppermute | solution.py:338
  80.5 8.2 %collective-permute-start.25 = (f32[6,16,256]{2,1,0:T(8,128)S(1)}, f32[6,16,256]{2,1,0:T(8,128)S(1)}, u32[]{:S(2)}, u32[]{:S(2)}) collective-permute-start(f32[6,16,256]{2,1,0:T(8,128)S(1)} %get-tuple-element.88), channel_id=1, source_target_pairs={{0,2},{1,3},{2,0},{3,1},{4,6},{5,7},{6,4},{7,5},{8,10},{9,11},{10,... | collective-permute-start | bytes 294920 | tf_op jit(solution)/shard_map/ppermute | solution.py:338
  80.5 8.9 %collective-permute-start.23 = (f32[6,16,256]{2,1,0:T(8,128)S(1)}, f32[6,16,256]{2,1,0:T(8,128)S(1)}, u32[]{:S(2)}, u32[]{:S(2)}) collective-permute-start(f32[6,16,256]{2,1,0:T(8,128)S(1)} %collective-permute-done.22.rest_3_), channel_id=1, source_target_pairs={{0,1},{1,0},{2,3},{3,2},{4,5},{5,4},{6,7},{7,6},{8,9},{9,8},{10,11... | collective-permute-start | bytes 294920 | tf_op jit(solution)/shard_map/ppermute | solution.py:338
  102.0 5.2 %collective-permute-start.39 = (f32[2,32,256]{2,1,0:T(8,128)S(1)}, f32[2,32,256]{2,1,0:T(8,128)S(1)}, u32[]{:S(2)}, u32[]{:S(2)}) collective-permute-start(f32[2,32,256]{2,1,0:T(8,128)S(1)} %get-tuple-element.99), channel_id=1, source_target_pairs={{0,24},{4,28},{8,16},{12,20},{16,8},{20,12},{24,0},{28,4},{1,25},{... | collective-permute-start | bytes 196616 | tf_op jit(solution)/shard_map/ppermute | solution.py:290
  107.2 23.0 %collective-permute-start.45 = (f32[6,32,256]{2,1,0:T(8,128)S(1)}, f32[6,32,256]{2,1,0:T(8,128)S(1)}, u32[]{:S(2)}, u32[]{:S(2)}) collective-permute-start(f32[6,32,256]{2,1,0:T(8,128)S(1)} %get-tuple-element.102.rest_3_), channel_id=1, source_target_pairs={{0,1},{1,0},{2,3},{3,2},{4,5},{5,4},{6,7},{7,6},{8,9},{9,8},{10,11... | collective-permute-start | bytes 589832 | tf_op jit(solution)/shard_map/ppermute | solution.py:338
  108.2 15.1 %collective-permute-start.40 = (f32[6,16,256]{2,1,0:T(8,128)S(1)}, f32[6,16,256]{2,1,0:T(8,128)S(1)}, u32[]{:S(2)}, u32[]{:S(2)}) collective-permute-start(f32[6,16,256]{2,1,0:T(8,128)S(1)} %get-tuple-element.100), channel_id=1, source_target_pairs={{0,2},{1,3},{2,0},{3,1},{4,6},{5,7},{6,4},{7,5},{8,10},{9,11},{10,... | collective-permute-start | bytes 294920 | tf_op jit(solution)/shard_map/ppermute | solution.py:338
  109.7 13.6 %collective-permute-start.42 = (f32[2,32,256]{2,1,0:T(8,128)S(1)}, f32[2,32,256]{2,1,0:T(8,128)S(1)}, u32[]{:S(2)}, u32[]{:S(2)}) collective-permute-start(f32[2,32,256]{2,1,0:T(8,128)S(1)} %get-tuple-element.96.rest_2_), channel_id=1, source_target_pairs={{0,2},{1,3},{2,0},{3,1},{4,6},{5,7},{6,4},{7,5},{8,10},{9,11},{10,... | collective-permute-start | bytes 196616 | tf_op jit(solution)/shard_map/ppermute | solution.py:338
  111.1 14.7 %collective-permute-start.36 = (f32[2,32,256]{2,1,0:T(8,128)S(1)}, f32[2,32,256]{2,1,0:T(8,128)S(1)}, u32[]{:S(2)}, u32[]{:S(2)}) collective-permute-start(f32[2,32,256]{2,1,0:T(8,128)S(1)} %get-tuple-element.96.rest_2_), channel_id=1, source_target_pairs={{0,3},{1,2},{2,1},{3,0},{4,7},{5,6},{6,5},{7,4},{8,11},{9,10},{10,... | collective-permute-start | bytes 196616 | tf_op jit(solution)/shard_map/ppermute | solution.py:338
  113.0 15.1 %collective-permute-start.46 = (f32[6,16,256]{2,1,0:T(8,128)S(1)}, f32[6,16,256]{2,1,0:T(8,128)S(1)}, u32[]{:S(2)}, u32[]{:S(2)}) collective-permute-start(f32[6,16,256]{2,1,0:T(8,128)S(1)} %get-tuple-element.101), channel_id=1, source_target_pairs={{0,3},{1,2},{2,1},{3,0},{4,7},{5,6},{6,5},{7,4},{8,11},{9,10},{10,... | collective-permute-start | bytes 294920 | tf_op jit(solution)/shard_map/ppermute | solution.py:338
  123.3 8.2 %collective-permute-start.43 = (f32[6,16,256]{2,1,0:T(8,128)S(1)}, f32[6,16,256]{2,1,0:T(8,128)S(1)}, u32[]{:S(2)}, u32[]{:S(2)}) collective-permute-start(f32[6,16,256]{2,1,0:T(8,128)S(1)} %get-tuple-element.101), channel_id=1, source_target_pairs={{0,2},{1,3},{2,0},{3,1},{4,6},{5,7},{6,4},{7,5},{8,10},{9,11},{10,... | collective-permute-start | bytes 294920 | tf_op jit(solution)/shard_map/ppermute | solution.py:338
  123.3 8.9 %collective-permute-start.41 = (f32[6,16,256]{2,1,0:T(8,128)S(1)}, f32[6,16,256]{2,1,0:T(8,128)S(1)}, u32[]{:S(2)}, u32[]{:S(2)}) collective-permute-start(f32[6,16,256]{2,1,0:T(8,128)S(1)} %collective-permute-done.40.rest_3_), channel_id=1, source_target_pairs={{0,1},{1,0},{2,3},{3,2},{4,5},{5,4},{6,7},{7,6},{8,9},{9,8},{10,11... | collective-permute-start | bytes 294920 | tf_op jit(solution)/shard_map/ppermute | solution.py:338
  150.0 23.0 %collective-permute-start.63 = (f32[6,32,256]{2,1,0:T(8,128)S(1)}, f32[6,32,256]{2,1,0:T(8,128)S(1)}, u32[]{:S(2)}, u32[]{:S(2)}) collective-permute-start(f32[6,32,256]{2,1,0:T(8,128)S(1)} %get-tuple-element.113.rest_3_), channel_id=1, source_target_pairs={{0,1},{1,0},{2,3},{3,2},{4,5},{5,4},{6,7},{7,6},{8,9},{9,8},{10,11... | collective-permute-start | bytes 589832 | tf_op jit(solution)/shard_map/ppermute | solution.py:338
  151.0 15.1 %collective-permute-start.58 = (f32[6,16,256]{2,1,0:T(8,128)S(1)}, f32[6,16,256]{2,1,0:T(8,128)S(1)}, u32[]{:S(2)}, u32[]{:S(2)}) collective-permute-start(f32[6,16,256]{2,1,0:T(8,128)S(1)} %get-tuple-element.111), channel_id=1, source_target_pairs={{0,2},{1,3},{2,0},{3,1},{4,6},{5,7},{6,4},{7,5},{8,10},{9,11},{10,... | collective-permute-start | bytes 294920 | tf_op jit(solution)/shard_map/ppermute | solution.py:338
  152.5 13.6 %collective-permute-start.60 = (f32[2,32,256]{2,1,0:T(8,128)S(1)}, f32[2,32,256]{2,1,0:T(8,128)S(1)}, u32[]{:S(2)}, u32[]{:S(2)}) collective-permute-start(f32[2,32,256]{2,1,0:T(8,128)S(1)} %get-tuple-element.107.rest_2_), channel_id=1, source_target_pairs={{0,2},{1,3},{2,0},{3,1},{4,6},{5,7},{6,4},{7,5},{8,10},{9,11},{10,... | collective-permute-start | bytes 196616 | tf_op jit(solution)/shard_map/ppermute | solution.py:338
  153.9 14.7 %collective-permute-start.54 = (f32[2,32,256]{2,1,0:T(8,128)S(1)}, f32[2,32,256]{2,1,0:T(8,128)S(1)}, u32[]{:S(2)}, u32[]{:S(2)}) collective-permute-start(f32[2,32,256]{2,1,0:T(8,128)S(1)} %get-tuple-element.107.rest_2_), channel_id=1, source_target_pairs={{0,3},{1,2},{2,1},{3,0},{4,7},{5,6},{6,5},{7,4},{8,11},{9,10},{10,... | collective-permute-start | bytes 196616 | tf_op jit(solution)/shard_map/ppermute | solution.py:338
  155.8 14.9 %collective-permute-start.64 = (f32[6,16,256]{2,1,0:T(8,128)S(1)}, f32[6,16,256]{2,1,0:T(8,128)S(1)}, u32[]{:S(2)}, u32[]{:S(2)}) collective-permute-start(f32[6,16,256]{2,1,0:T(8,128)S(1)} %get-tuple-element.112), channel_id=1, source_target_pairs={{0,3},{1,2},{2,1},{3,0},{4,7},{5,6},{6,5},{7,4},{8,11},{9,10},{10,... | collective-permute-start | bytes 294920 | tf_op jit(solution)/shard_map/ppermute | solution.py:338
  166.1 8.2 %collective-permute-start.61 = (f32[6,16,256]{2,1,0:T(8,128)S(1)}, f32[6,16,256]{2,1,0:T(8,128)S(1)}, u32[]{:S(2)}, u32[]{:S(2)}) collective-permute-start(f32[6,16,256]{2,1,0:T(8,128)S(1)} %get-tuple-element.112), channel_id=1, source_target_pairs={{0,2},{1,3},{2,0},{3,1},{4,6},{5,7},{6,4},{7,5},{8,10},{9,11},{10,... | collective-permute-start | bytes 294920 | tf_op jit(solution)/shard_map/ppermute | solution.py:338
  166.1 8.9 %collective-permute-start.59 = (f32[6,16,256]{2,1,0:T(8,128)S(1)}, f32[6,16,256]{2,1,0:T(8,128)S(1)}, u32[]{:S(2)}, u32[]{:S(2)}) collective-permute-start(f32[6,16,256]{2,1,0:T(8,128)S(1)} %collective-permute-done.58.rest_3_), channel_id=1, source_target_pairs={{0,1},{1,0},{2,3},{3,2},{4,5},{5,4},{6,7},{7,6},{8,9},{9,8},{10,11... | collective-permute-start | bytes 294920 | tf_op jit(solution)/shard_map/ppermute | solution.py:338
  (41 other events, 147.7 us)
